TPU v7x, 32 devices: a whole 2x2x4 slice. The times are simulated.
32 devices in a mesh: dp: 8 (over z, core), graph: 4 (over y, x).
Axes of the slice: x: 2, y: 2, z: 4, core: 2. Of those that a mesh axis runs over, the one named last changes fastest.
Arguments:
- edge_feats: bfloat16 [32768, 512], P(('dp', 'graph')), may hold values from -6 to 6
- cotangent: bfloat16 [32768, 512], P(('dp', 'graph')), may hold values from -6 to 6
- angle_basis: bfloat16 [16, 262144], P(None, ('dp', 'graph')), may hold values from -6 to 6
- source_edge: int32 [262144], P(('dp', 'graph')), may hold values from 0 to 4095
- target_edge: int32 [262144], P(('dp', 'graph')), may hold values from 0 to 1023
- pair_weight: bfloat16 [512, 512], P('dp'), may hold values from -0.25 to 0.25
- down_weight: bfloat16 [512, 64], P('dp'), may hold values from -0.25 to 0.25
- basis_weight: bfloat16 [16, 64], P('dp'), may hold values from -1.5 to 1.5
- up_weight: bfloat16 [64, 512], P('dp'), may hold values from -0.75 to 0.75
- res_first: bfloat16 [512, 512], P('dp'), may hold values from -0.25 to 0.25
- res_second: bfloat16 [512, 512], P('dp'), may hold values from -0.25 to 0.25
Outputs:
- edge_grad: bfloat16 [32768, 512], P(('dp', 'graph'))
- pair_grad: float32 [512, 512], P('dp')
- down_grad: float32 [512, 64], P('dp')
- basis_grad: float32 [16, 64], P('dp')
- up_grad: float32 [64, 512], P('dp')
- first_grad: float32 [512, 512], P('dp')
- second_grad: float32 [512, 512], P('dp')
Inputs may be any that keep to these rules, and one draw needn't show every extreme that they name: source_edge[t] may name any edge of the 4 devices of the triplet's group. target_edge[t] names an edge of the triplet's own device.
All inputs are finite; a program needn't handle non-finite values.
Results may differ from a plain program's by a relative error of at most 0.013.
Values may be sent and summed in bfloat16 or wider, within the bound.
A program may use at most 64 MiB of HBM per device.

v0:
```python
import math

import jax
import jax.numpy as jnp
from jax import lax
from jax.sharding import PartitionSpec as P


def silu_slope(value):
    sig = jax.nn.sigmoid(value)
    return sig * (1.0 + value * (1.0 - sig))


def on_device(
    edge_feats,
    cotangent,
    angle_basis,
    source_edge,
    target_edge,
    pair_weight,
    down_weight,
    basis_weight,
    up_weight,
    res_first,
    res_second,
):
    f32 = jnp.float32
    bf16 = jnp.bfloat16
    scale = math.sqrt(0.5)
    w_pair, w_down, w_basis, w_up, w_first, w_second = (
        lax.all_gather(pair_weight, "dp", axis=0, tiled=True),
        lax.all_gather(down_weight, "dp", axis=0, tiled=True),
        lax.all_gather(basis_weight, "dp", axis=0, tiled=True),
        lax.all_gather(up_weight, "dp", axis=0, tiled=True),
        lax.all_gather(res_first, "dp", axis=0, tiled=True),
        lax.all_gather(res_second, "dp", axis=0, tiled=True),
    )
    edge_rows = edge_feats.shape[0]
    width_trip = w_down.shape[1]
    z_one = jnp.dot(edge_feats, w_pair, preferred_element_type=f32)
    hidden = jax.nn.silu(z_one).astype(bf16)
    down_t = jnp.einsum("ed,dk->ke", hidden, w_down, preferred_element_type=f32).astype(bf16)
    group_down = lax.all_gather(down_t, "graph", axis=1, tiled=True)
    group_cols = group_down.shape[1]
    coeff = jnp.einsum("nk,nt->kt", w_basis, angle_basis, preferred_element_type=f32)
    down_in = jnp.take(group_down, source_edge, axis=1).astype(f32)
    agg_t = (
        jnp.zeros((width_trip, edge_rows), f32).at[:, target_edge].add(down_in * coeff).astype(bf16)
    )
    z_two = jnp.einsum("ke,kd->ed", agg_t, w_up, preferred_element_type=f32)
    mixed = jax.nn.silu(z_two).astype(bf16)
    z_three = jnp.dot(mixed, w_first, preferred_element_type=f32)
    inner = jax.nn.silu(z_three).astype(bf16)
    z_four = jnp.dot(inner, w_second, preferred_element_type=f32)
    dz_four = (scale * cotangent.astype(f32) * silu_slope(z_four)).astype(bf16)
    dz_three = (
        jnp.einsum("ed,fd->ef", dz_four, w_second, preferred_element_type=f32) * silu_slope(z_three)
    ).astype(bf16)
    dmixed = scale * cotangent.astype(f32) + jnp.einsum(
        "ed,fd->ef", dz_three, w_first, preferred_element_type=f32
    )
    dz_two = (dmixed * silu_slope(z_two)).astype(bf16)
    dagg_t = jnp.einsum("kd,ed->ke", w_up, dz_two, preferred_element_type=f32)
    dagg_out = jnp.take(dagg_t, target_edge, axis=1)
    dcoeff = (dagg_out * down_in).astype(bf16)
    partial_down = jnp.zeros((width_trip, group_cols), f32).at[:, source_edge].add(dagg_out * coeff)
    ddown_t = lax.psum_scatter(partial_down, "graph", scatter_dimension=1, tiled=True).astype(bf16)
    second_local = jnp.einsum("ed,ef->df", inner, dz_four, preferred_element_type=f32)
    first_local = jnp.einsum("ed,ef->df", mixed, dz_three, preferred_element_type=f32)
    up_local = jnp.einsum("ke,ed->kd", agg_t, dz_two, preferred_element_type=f32)
    basis_local = jnp.einsum("nt,kt->nk", angle_basis, dcoeff, preferred_element_type=f32)
    down_local = jnp.einsum("ed,ke->dk", hidden, ddown_t, preferred_element_type=f32)
    dz_one = (
        jnp.einsum("ke,dk->ed", ddown_t, w_down, preferred_element_type=f32) * silu_slope(z_one)
    ).astype(bf16)
    pair_local = jnp.einsum("ed,ef->df", edge_feats, dz_one, preferred_element_type=f32)
    edge_grad = jnp.einsum("ef,df->ed", dz_one, w_pair, preferred_element_type=f32).astype(bf16)
    locals_all = (pair_local, down_local, basis_local, up_local, first_local, second_local)
    data_count = lax.axis_size("dp")
    packed = jnp.concatenate([item.reshape(data_count, -1) for item in locals_all], axis=1).reshape(
        -1
    )
    rows_sum = lax.psum_scatter(packed, "dp", scatter_dimension=0, tiled=True)
    shares = lax.psum(rows_sum, "graph")
    outputs = []
    offset = 0
    for item in locals_all:
        share_rows = item.shape[0] // data_count
        length = share_rows * item.shape[1]
        outputs.append(shares[offset : offset + length].reshape(share_rows, item.shape[1]))
        offset = offset + length
    return (edge_grad, outputs[0], outputs[1], outputs[2], outputs[3], outputs[4], outputs[5])


def solution(mesh):
    return jax.shard_map(
        on_device,
        mesh=mesh,
        in_specs=(
            P(("dp", "graph"), None),
            P(("dp", "graph"), None),
            P(None, ("dp", "graph")),
            P(("dp", "graph")),
            P(("dp", "graph")),
            P("dp", None),
            P("dp", None),
            P("dp", None),
            P("dp", None),
            P("dp", None),
            P("dp", None),
        ),
        out_specs=(
            P(("dp", "graph"), None),
            P("dp", None),
            P("dp", None),
            P("dp", None),
            P("dp", None),
            P("dp", None),
            P("dp", None),
        ),
        check_vma=False,
    )
```

profile of v0, /device:TPU:0, one launch (start us, length us, event | category | flops | bytes accessed | tf_op | source)
XLA Modules:
  0.0 480.9 jit_solution(740085253470354246)
XLA Ops:
  7.2 0.8 broadcast_clamp_fusion.1
  8.1 0.8 compare_and_fusion
  8.9 0.8 broadcast_clamp_fusion
  9.7 13.6 %all-gather = bf16[8,2,64]{2,1,0:T(2,128)(2,1)S(1)} all-gather(bf16[1,2,64]{2,1,0:T(2,128)(2,1)} %bitcast.59), channel_id=1, replica_groups=mesh['dp'=8,'graph'=4] {'dp'}, dimensions={0}, use_global_device_ids=true | all-gather | bytes 2304 | tf_op jit(solution)/shard_map/all_gather | solution.py:33
  23.3 14.2 %all_gather.25 = bf16[64,512]{1,0:T(8,128)(2,1)S(1)} all-gather(bf16[8,512]{1,0:T(8,128)(2,1)} %param.19), channel_id=1, replica_groups=mesh['dp'=8,'graph'=4] {'dp'}, dimensions={0}, use_global_device_ids=true | all-gather | bytes 73728 | tf_op jit(solution)/shard_map/all_gather | solution.py:34
  37.5 14.2 %all_gather.22 = bf16[512,64]{1,0:T(8,128)(2,1)S(1)} all-gather(bf16[64,64]{1,0:T(8,128)(2,1)} %param.17), channel_id=1, replica_groups=mesh['dp'=8,'graph'=4] {'dp'}, dimensions={0}, use_global_device_ids=true | all-gather | bytes 73728 | tf_op jit(solution)/shard_map/all_gather | solution.py:32
  51.7 15.1 %all_gather.21 = bf16[512,512]{1,0:T(8,128)(2,1)S(1)} all-gather(bf16[64,512]{1,0:T(8,128)(2,1)} %param.16), channel_id=1, replica_groups=mesh['dp'=8,'graph'=4] {'dp'}, dimensions={0}, use_global_device_ids=true | all-gather | bytes 589824 | tf_op jit(solution)/shard_map/all_gather | solution.py:31
  66.8 16.0 %all_gather.26 = bf16[512,512]{1,0:T(8,128)(2,1)} all-gather(bf16[64,512]{1,0:T(8,128)(2,1)} %param.20), channel_id=1, replica_groups=mesh['dp'=8,'graph'=4] {'dp'}, dimensions={0}, use_global_device_ids=true | all-gather | bytes 589824 | tf_op jit(solution)/shard_map/all_gather | solution.py:35
  82.8 16.1 %all_gather.27 = bf16[512,512]{1,0:T(8,128)(2,1)} all-gather(bf16[64,512]{1,0:T(8,128)(2,1)} %param.21), channel_id=1, replica_groups=mesh['dp'=8,'graph'=4] {'dp'}, dimensions={0}, use_global_device_ids=true | all-gather | bytes 589824 | tf_op jit(solution)/shard_map/all_gather | solution.py:36
  98.8 2.3 multiply_convert_fusion.6
  101.1 0.4 fusion.3
  101.6 0.5 copy-done.5
  102.1 10.3 %all_gather.23 = bf16[64,4096]{1,0:T(8,128)(2,1)S(1)} all-gather(bf16[64,1024]{1,0:T(8,128)(2,1)S(1)} %fusion.3), channel_id=1, replica_groups=mesh['dp'=8,'graph'=4] {'graph'}, dimensions={1}, use_global_device_ids=true | all-gather | bytes 655360 | tf_op jit(solution)/shard_map/all_gather | solution.py:43
  112.4 0.5 copy.32
  112.9 29.2 %gather_fusion = bf16[8192,64]{1,0:T(8,128)(2,1)} fusion(bf16[64,4096]{0,1:T(8,128)(2,1)S(1)} %copy.32, s32[8192]{0:T(1024)S(1)} %get-tuple-element.14), kind=kCustom, calls=%fused_computation | custom fusion | bytes 2129920 | tf_op jit(solution)/shard_map/jit(_take)/gather | solution.py:46
  142.1 2.7 copy.33
  144.8 0.4 fusion.23
  145.3 1.4 copy-done.1
  146.9 2.7 copy.34
  149.6 44.6 %scatter_custom_fusion = f32[64,1024]{0,1:T(8,128)S(1)} fusion(s32[8192]{0:T(1024)S(1)} %get-tuple-element.13, f32[8192,64]{1,0:T(8,128)} %copy.34, f32[]{:T(128)} %constant.22.clone.1), kind=kCustom, calls=%fused_computation.33 | custom fusion | flops 524288 | bytes 262656 | tf_op jit(solution)/shard_map/scatter-add | solution.py:48
  194.3 0.7 multiply_convert_fusion.5
  195.5 1.0 multiply_convert_fusion.4
  196.9 1.3 multiply_convert_fusion.3
  198.2 1.2 multiply_convert_fusion.2
  199.4 1.3 multiply_convert_fusion.1
  200.7 1.0 copy-done.8
  202.3 27.7 %gather_fusion.1 = f32[8192,64]{1,0:T(8,128)} fusion(f32[64,1024]{0,1:T(8,128)S(1)} %copy.35, s32[8192]{0:T(1024)S(1)} %get-tuple-element.12), kind=kCustom, calls=%fused_computation.1 | custom fusion | bytes 4227072 | tf_op jit(solution)/shard_map/jit(_take)/gather | solution.py:64
  230.1 4.0 copy.36
  234.1 3.2 fusion
  237.3 3.8 copy.37
  241.1 45.9 %scatter_custom_fusion.1 = f32[64,4096]{0,1:T(8,128)} fusion(s32[8192]{0:T(1024)S(1)} %get-tuple-element.15, f32[8192,64]{1,0:T(8,128)} %copy.37, f32[]{:T(128)} %constant.22.clone.1), kind=kCustom, calls=%fused_computation.28 | custom fusion | flops 524288 | bytes 1049088 | tf_op jit(solution)/shard_map/scatter-add | solution.py:66
  287.6 2.3 fusion.25
  289.9 1.2 reshape.84
  291.5 2.9 fusion.24
  294.4 2.6 reshape.83
  297.0 1.8 convolution_bitcast_fusion.2
  298.9 20.7 %reduce-scatter.2.cloned.1.call-done = f32[64,1024]{0,1:T(8,128)} async-done(((f32[64,4096]{0,1:T(8,128)}), f32[64,1024]{0,1:T(8,128)}) %reduce-scatter.2.cloned.1.call-update) | async-done | bytes 262160 | tf_op jit(solution)/shard_map/reduce_scatter | solution.py:67
  319.6 1.9 fusion.12
  321.6 2.4 multiply_convert_fusion
  324.1 1.0 copy-done.20
  325.1 0.7 convolution_bitcast_fusion
  326.1 1.2 reshape.79
  327.3 2.4 constant_dynamic-update-slice_fusion.5
  329.7 0.6 constant_dynamic-update-slice_fusion.4
  330.3 0.6 constant_dynamic-update-slice_fusion.3
  330.9 0.7 constant_dynamic-update-slice_fusion.2
  331.6 1.0 constant_dynamic-update-slice_fusion.1
  332.7 1.0 constant_dynamic-update-slice_fusion
  333.7 4.2 reshape.85
  338.0 0.6 copy-done.19
  338.5 0.6 dynamic-slice
  339.8 80.9 %all-reduce.6.cloned.1.call-done = f32[852992]{0:T(1024)} async-done(((f32[852992]{0:T(1024)}), f32[852992]{0:T(1024)}) %all-reduce.6.cloned.1.call-update) | async-done | bytes 3411984
  420.6 1.9 dynamic-slice.1
  422.6 1.7 convolution_convert_fusion
  424.3 43.6 %all-reduce.4.cloned.1.call-done = f32[106624]{0:T(1024)} async-done(((f32[106624]{0:T(1024)}), f32[106624]{0:T(1024)}) %all-reduce.4.cloned.1.call-update) | async-done | bytes 426512 | tf_op jit(solution)/shard_map/psum | solution.py:84
  467.9 0.7 slice.46
  468.6 0.6 reshape.88
  469.2 1.1 fusion.21
  470.3 0.7 reshape.91
  471.0 0.7 fusion.22
  471.7 0.6 reshape.89
  472.3 0.7 reshape.87
  473.0 0.7 reshape.90
  473.7 0.7 reshape.86
  (63 shorter events, 3.5 us)
Async XLA Ops:
  7.2 91.7 %copy-start = (bf16[1024,512]{1,0:T(8,128)(2,1)S(1)}, bf16[1024,512]{1,0:T(8,128)(2,1)}, u32[]{:S(2)}) copy-start(bf16[1024,512]{1,0:T(8,128)(2,1)} %param.11) | copy-start | bytes 3145732
  7.2 312.4 %reduce-scatter.2.cloned.1.call-start = ((), (), s32[]{:S(2)}) async-start(), calls=%async_computation.1 | async-start | bytes 2621440 | tf_op jit(solution)/shard_map/reduce_scatter | solution.py:67
  66.8 34.3 %copy-start.13 = (bf16[512,512]{1,0:T(8,128)(2,1)}, bf16[512,512]{1,0:T(8,128)(2,1)S(1)}, u32[]{:S(2)}) copy-start(bf16[512,512]{1,0:T(8,128)(2,1)S(1)} %all_gather.21) | copy-start | bytes 1572868
  101.1 1.0 copy-start.5
  142.1 2.7 copy-start.17
  144.8 1.8 copy-start.4
  145.3 1.4 copy-start.1
  194.2 0.8 copy-start.10
  194.2 1.2 copy-start.15
  195.1 1.4 copy-start.22
  195.5 1.0 copy-start.16
  195.5 1.4 copy-start.18
  196.5 1.7 copy-start.25
  198.2 1.2 copy-start.26
  199.4 1.3 copy-start.24
  200.7 1.0 copy-start.8
  230.1 4.0 copy-start.2
  241.1 46.2 %copy-start.9 = (bf16[1024,512]{1,0:T(8,128)(2,1)S(1)}, bf16[1024,512]{1,0:T(8,128)(2,1)}, u32[]{:S(2)}) copy-start(bf16[1024,512]{1,0:T(8,128)(2,1)} %copy-done.8) | copy-start | bytes 3145732
  241.1 46.2 %copy-start.11 = (f32[64,1024]{0,1:T(8,128)S(1)}, f32[64,1024]{0,1:T(8,128)}, u32[]{:S(2)}) copy-start(f32[64,1024]{0,1:T(8,128)} %copy-done.10) | copy-start | bytes 786436
  287.0 133.7 %all-reduce.6.cloned.1.call-start = ((), (), s32[]{:S(2)}) async-start(), calls=%async_computation.3 | async-start | bytes 6823936
  289.9 1.6 copy-start.23
  294.4 2.6 copy-start.3
  319.6 2.0 copy-start.12
  324.1 1.0 copy-start.20
  326.1 5.5 %copy-start.7 = (f32[8,32768]{1,0:T(8,128)S(1)}, f32[8,32768]{1,0:T(8,128)}, u32[]{:S(2)}) copy-start(f32[8,32768]{1,0:T(8,128)} %reshape.83) | copy-start | bytes 3145732
  327.3 5.3 %copy-start.6 = (f32[8,32768]{1,0:T(8,128)S(1)}, f32[8,32768]{1,0:T(8,128)}, u32[]{:S(2)}) copy-start(f32[8,32768]{1,0:T(8,128)} %reshape.84) | copy-start | bytes 3145732
  337.9 0.7 copy-start.19
  337.9 84.7 %copy-start.14 = (bf16[512,512]{1,0:T(8,128)(2,1)S(1)}, bf16[512,512]{1,0:T(8,128)(2,1)}, u32[]{:S(2)}) copy-start(bf16[512,512]{1,0:T(8,128)(2,1)} %copy-done.13) | copy-start | bytes 1572868
  337.9 84.7 %copy-start.21 = (bf16[1024,512]{1,0:T(8,128)(2,1)S(1)}, bf16[1024,512]{1,0:T(8,128)(2,1)}, u32[]{:S(2)}) copy-start(bf16[1024,512]{1,0:T(8,128)(2,1)} %copy-done.20) | copy-start | bytes 3145732
  337.9 130.0 %all-reduce.4.cloned.1.call-start = ((), (), s32[]{:S(2)}) async-start(), calls=%async_computation.2 | async-start | bytes 860160 | tf_op jit(solution)/shard_map/psum | solution.py:84
Sparse Core Ops, SparseCore 0:
  287.1 32.5 reduce-scatter.1
  338.0 82.5 all-reduce.5
  423.6 44.2 all-reduce.3
where the time goes:
time: 482 us; the launch traced here: 481 us
  waiting for transfers between devices  145 us (30%)
  local copies, waits for them, and re-layouts  102 us (21%)
  blocking collectives  99.5 us (21%)
  other arithmetic  96.3 us (20%)
  matrix products  23.1 us (5%)
  between operations  14.7 us (3%)
    unnamed x4, waiting for transfers between devices  80.9 us
    scatter-add x1, other arithmetic, on_device(): jnp.zeros((width_trip, group_cols), f32).at[:, source_edge]  45.9 us
    scatter-add x1, other arithmetic, on_device(): jnp.zeros((width_trip, edge_rows), f32).at[:, target_edge]  44.6 us
    psum x1, waiting for transfers between devices, on_device(): shares = lax.psum(rows_sum, 'graph')  43.6 us
    gather x2, local copies, waits for them, and re-layouts, on_device(): down_in = jnp.take(group_down, source_edge, axis=1).astype(f32)  32 us
    gather x2, local copies, waits for them, and re-layouts, on_device(): dagg_out = jnp.take(dagg_t, target_edge, axis=1)  31.8 us
    reduce_scatter x1, waiting for transfers between devices, on_device(): lax.psum_scatter(partial_down, 'graph', scatter_dimension=1, tiled=True)  20.7 us
    all_gather x1, blocking collectives, on_device(): lax.all_gather(res_second, 'dp', axis=0, tiled=True)  16.1 us
  transfers between devices with their start and end apart: 3, of which 3 were waited for; matrix products, arithmetic and copies ran while one was open for 3% of the time, Pallas kernels for 0%

commit v1 on v0

v1 whole, which is shorter than its diff:
```python
import functools
import math

import jax
import jax.numpy as jnp
from jax import lax
from jax.experimental import pallas as pl
from jax.experimental.pallas import tpu as pltpu
from jax.sharding import PartitionSpec as P

MESH = pl.DeviceIdType.MESH
F32 = jnp.float32
BF16 = jnp.bfloat16
VM = pl.BlockSpec(memory_space=pltpu.VMEM)
SUB = 256
TILE = 1024


def remote(src, dst, send, recv, target):
    return pltpu.make_async_remote_copy(
        src_ref=src,
        dst_ref=dst,
        send_sem=send,
        recv_sem=recv,
        device_id=target,
        device_id_type=MESH,
    )


def silu_slope(value):
    sig = jax.nn.sigmoid(value)
    return sig * (1.0 + value * (1.0 - sig))


def gather_kernel(n, count, *refs):
    ins, outs = refs[:count], refs[count : 2 * count]
    send, recv = refs[2 * count :]
    half = n // 2
    dp = lax.axis_index("dp")
    pos = dp // 2
    core = dp % 2
    partner = dp + 1 - 2 * core
    has_up = pos < half - 1
    has_down = pos > 0
    barrier = pltpu.get_barrier_semaphore()

    @pl.when(has_up)
    def _():
        pl.semaphore_signal(barrier, inc=1, device_id={"dp": dp + 2}, device_id_type=MESH)

    @pl.when(has_down)
    def _():
        pl.semaphore_signal(barrier, inc=1, device_id={"dp": dp - 2}, device_id_type=MESH)

    pl.semaphore_signal(barrier, inc=1, device_id={"dp": partner}, device_id_type=MESH)

    pl.semaphore_wait(barrier, 1 + has_up.astype(jnp.int32) + has_down.astype(jnp.int32))

    def copy(w, src, shard, way, target):
        return remote(
            src, outs[w].at[shard], send.at[shard, way, w], recv.at[shard, w], {"dp": target}
        )

    for w in range(count):

        @pl.when(has_up)
        def _():
            copy(w, ins[w], dp, 0, dp + 2).start()

        @pl.when(has_down)
        def _():
            copy(w, ins[w], dp, 1, dp - 2).start()

        copy(w, ins[w], dp, 2, partner).start()
    for w in range(count):
        outs[w][dp] = ins[w][...]
    for k in range(1, half):
        for w in range(count):

            @pl.when(pos >= k)
            def _():
                shard = dp - 2 * k
                block = outs[w].at[shard]
                copy(w, block, shard, 2, partner).wait_recv()

                @pl.when(has_up)
                def _():
                    copy(w, block, shard, 0, dp + 2).start()

                copy(w, block, shard, 2, partner).start()

            @pl.when(pos + k < half)
            def _():
                shard = dp + 2 * k
                block = outs[w].at[shard]
                copy(w, block, shard, 2, partner).wait_recv()

                @pl.when(has_down)
                def _():
                    copy(w, block, shard, 1, dp - 2).start()

                copy(w, block, shard, 2, partner).start()

    for w in range(count):
        for q in range(half):
            shard = 2 * q + 1 - core
            copy(w, outs[w].at[shard], shard, 2, partner).wait_recv()
            mine = 2 * q + core
            copy(w, outs[w].at[mine], mine, 2, partner).wait_send()

            @pl.when(jnp.logical_and(pos >= q, has_up))
            def _():
                copy(w, outs[w].at[mine], mine, 0, dp + 2).wait_send()

            @pl.when(jnp.logical_and(pos <= q, has_down))
            def _():
                copy(w, outs[w].at[mine], mine, 1, dp - 2).wait_send()


def gather_weights(n, weights):
    count = len(weights)
    return pl.pallas_call(
        functools.partial(gather_kernel, n, count),
        out_shape=[jax.ShapeDtypeStruct((n,) + w.shape, w.dtype) for w in weights],
        in_specs=[VM] * count,
        out_specs=[VM] * count,
        scratch_shapes=[
            pltpu.SemaphoreType.DMA((n, 3, count)),
            pltpu.SemaphoreType.DMA((n, count)),
        ],
        compiler_params=pltpu.CompilerParams(collective_id=0, has_side_effects=True),
        name="gather_weights",
    )(*weights)


def greet_graph(groups, me):
    barrier = pltpu.get_barrier_semaphore()
    for k in range(1, groups):
        pl.semaphore_signal(
            barrier, inc=1, device_id={"graph": (me + k) % groups}, device_id_type=MESH
        )
    pl.semaphore_wait(barrier, groups - 1)


def spread_kernel(groups, in_ref, out_ref, send, recv):
    me = lax.axis_index("graph")
    greet_graph(groups, me)
    copies = []
    for k in range(1, groups):
        cp = remote(
            in_ref, out_ref.at[me], send.at[k], recv.at[k], {"graph": (me + k) % groups}
        )
        cp.start()
        copies.append(cp)
    out_ref[me] = in_ref[...]
    for cp in copies:
        cp.wait()


def spread_down(groups, block):
    return pl.pallas_call(
        functools.partial(spread_kernel, groups),
        out_shape=jax.ShapeDtypeStruct((groups,) + block.shape, block.dtype),
        in_specs=[VM],
        out_specs=VM,
        scratch_shapes=[pltpu.SemaphoreType.DMA((groups,))] * 2,
        compiler_params=pltpu.CompilerParams(collective_id=1, has_side_effects=True),
        name="spread_down",
    )(block)


def collect_kernel(groups, in_ref, out_ref, landed, send, recv):
    me = lax.axis_index("graph")
    greet_graph(groups, me)
    copies = []
    for k in range(1, groups):
        peer = (me + k) % groups
        cp = remote(in_ref.at[peer], landed.at[k], send.at[k], recv.at[k], {"graph": peer})
        cp.start()
        copies.append(cp)
    for cp in copies:
        cp.wait()
    total = in_ref[me].astype(F32)
    for k in range(1, groups):
        total = total + landed[k].astype(F32)
    out_ref[...] = total.astype(out_ref.dtype)


def collect_down(groups, partial):
    shape = partial.shape[1:]
    return pl.pallas_call(
        functools.partial(collect_kernel, groups),
        out_shape=jax.ShapeDtypeStruct(shape, BF16),
        in_specs=[VM],
        out_specs=VM,
        scratch_shapes=[pltpu.VMEM(partial.shape, partial.dtype)]
        + [pltpu.SemaphoreType.DMA((groups,))] * 2,
        compiler_params=pltpu.CompilerParams(collective_id=2, has_side_effects=True),
        name="collect_down",
    )(partial)


def total_kernel(n, groups, kinds, *refs):
    count = len(kinds)
    ins, outs = refs[:count], refs[count : 2 * count]
    pos_in = 2 * count
    scratch = []
    for large in kinds:
        size = 7 if large else 5
        scratch.append(refs[pos_in : pos_in + size])
        pos_in += size
    a_send, a_recv, b_send, b_recv, c_send, c_recv, d_send, d_recv = refs[pos_in:]
    half = n // 2
    dp = lax.axis_index("dp")
    me = lax.axis_index("graph")
    pos = dp // 2
    core = dp % 2
    partner = dp + 1 - 2 * core
    barrier = pltpu.get_barrier_semaphore()
    pl.semaphore_signal(barrier, inc=1, device_id={"dp": partner}, device_id_type=MESH)
    for k in range(1, groups):
        pl.semaphore_signal(
            barrier, inc=1, device_id={"graph": (me + k) % groups}, device_id_type=MESH
        )
    for k in range(1, half):
        pl.semaphore_signal(
            barrier,
            inc=1,
            device_id={"dp": (pos + k) % half * 2 + core},
            device_id_type=MESH,
        )
    pl.semaphore_wait(barrier, groups + half - 1)

    sent = []

    def send_all(copies):
        for cp in copies:
            cp.start()
        sent.extend(copies)
        return copies

    first = []
    for w in range(count):
        first.append(
            send_all(
                [
                    remote(
                        ins[w].at[2 * q + 1 - core],
                        scratch[w][0].at[q],
                        a_send.at[w, q],
                        a_recv.at[w, q],
                        {"dp": partner},
                    )
                    for q in range(half)
                ]
            )
        )
    second = []
    for w, large in enumerate(kinds):
        got, summed = scratch[w][0], scratch[w][1]
        for q in range(half):
            first[w][q].wait_recv()
            value = ins[w][2 * q + core].astype(F32) + got[q].astype(F32)
            if large:
                summed[:, q] = value.astype(summed.dtype)
            else:
                summed[q] = value.astype(summed.dtype)
        if large:
            second.append(
                send_all(
                    [
                        remote(
                            summed.at[(me + k) % groups],
                            scratch[w][5].at[k],
                            b_send.at[w, k],
                            b_recv.at[w, k],
                            {"graph": (me + k) % groups},
                        )
                        for k in range(1, groups)
                    ]
                )
            )
        else:
            second.append([])
    third = []
    for w, large in enumerate(kinds):
        if large:
            for cp in second[w]:
                cp.wait_recv()
            value = scratch[w][1][me].astype(F32)
            for k in range(1, groups):
                value = value + scratch[w][5][k].astype(F32)
            part = scratch[w][6]
            part[...] = value.astype(part.dtype)
        else:
            part = scratch[w][1]
        third.append(
            send_all(
                [
                    remote(
                        part.at[(pos + k) % half],
                        scratch[w][2].at[k],
                        c_send.at[w, k],
                        c_recv.at[w, k],
                        {"dp": (pos + k) % half * 2 + core},
                    )
                    for k in range(1, half)
                ]
            )
        )
    fourth = []
    for w, large in enumerate(kinds):
        part = scratch[w][6] if large else scratch[w][1]
        for cp in third[w]:
            cp.wait_recv()
        value = part[pos].astype(F32)
        for k in range(1, half):
            value = value + scratch[w][2][k].astype(F32)
        done = scratch[w][3]
        done[...] = value.astype(done.dtype)
        fourth.append(
            send_all(
                [
                    remote(
                        done,
                        scratch[w][4].at[me],
                        d_send.at[w, k],
                        d_recv.at[w, k],
                        {"graph": (me + k) % groups},
                    )
                    for k in range(1, groups)
                ]
            )
        )
        scratch[w][4][me] = value.astype(done.dtype)
    for w, large in enumerate(kinds):
        for cp in fourth[w]:
            cp.wait_recv()
        landed = scratch[w][4]
        if large:
            outs[w][...] = landed[...].astype(F32)
        else:
            value = landed[0].astype(F32)
            for g in range(1, groups):
                value = value + landed[g].astype(F32)
            outs[w][...] = value
    for cp in sent:
        cp.wait_send()


def total_grads(n, groups, grads, kinds):
    half = n // 2
    shapes, scratch = [], []
    for item, large in zip(grads, kinds):
        tail = item.shape[2:] if large else item.shape[1:]
        kind = item.dtype
        shapes.append(jax.ShapeDtypeStruct(((groups,) if large else ()) + tail, F32))
        scratch.append(pltpu.VMEM((half,) + item.shape[1:], kind))
        scratch.append(
            pltpu.VMEM(((groups, half) + tail) if large else ((half,) + tail), kind)
        )
        scratch.append(pltpu.VMEM((half,) + tail, kind))
        scratch.append(pltpu.VMEM(tail, kind))
        scratch.append(pltpu.VMEM((groups,) + tail, kind))
        if large:
            scratch.append(pltpu.VMEM((groups, half) + tail, kind))
            scratch.append(pltpu.VMEM((half,) + tail, kind))
    count = len(grads)
    sems = []
    for width in (half, groups, half, groups):
        sems += [pltpu.SemaphoreType.DMA((count, width))] * 2
    return pl.pallas_call(
        functools.partial(total_kernel, n, groups, kinds),
        out_shape=shapes,
        in_specs=[VM] * count,
        out_specs=[VM] * count,
        scratch_shapes=scratch + sems,
        compiler_params=pltpu.CompilerParams(collective_id=3, has_side_effects=True),
        name="total_grads",
    )(*grads)


def one_hot(size, row):
    spots = lax.broadcasted_iota(jnp.int32, (size, row.shape[1]), 0)
    return jnp.where(spots == row, 1.0, 0.0).astype(BF16)


def pick(stack, owner, groups, width):
    value = jnp.where(owner == 0, stack[:width], 0.0)
    for g in range(1, groups):
        value = value + jnp.where(owner == g, stack[g * width : (g + 1) * width], 0.0)
    return value


def place(value, owner, groups):
    return jnp.concatenate(
        [jnp.where(owner == g, value, 0.0).astype(BF16) for g in range(groups)], axis=0
    )


def dot(a, b, dims):
    return lax.dot_general(a, b, (dims, ((), ())), preferred_element_type=F32)


NN = ((1,), (0,))
NT = ((1,), (1,))
TN = ((0,), (0,))


def forward_kernel(
    groups, edges, width, src_ref, tgt_ref, basis_ref, wb_ref, table_ref, agg_ref, din_ref, acc
):
    step = pl.program_id(0)
    subs = edges // SUB

    @pl.when(step == 0)
    def _():
        acc[...] = jnp.zeros_like(acc)

    src = src_ref[...]
    tgt = tgt_ref[...]
    owner = src // edges
    stack = dot(table_ref[...], one_hot(edges, src - owner * edges), NN)
    down_in = pick(stack, owner, groups, width)
    din_ref[...] = down_in.astype(BF16)
    coeff = dot(wb_ref[...], basis_ref[...], TN)
    high = tgt // SUB
    acc[...] += dot(place(down_in * coeff, high, subs), one_hot(SUB, tgt - high * SUB), NT)

    @pl.when(step == pl.num_programs(0) - 1)
    def _():
        for h in range(subs):
            agg_ref[:, h * SUB : (h + 1) * SUB] = acc[h * width : (h + 1) * width, :].astype(BF16)


def forward_triplets(groups, edges, src, tgt, basis, w_basis, table):
    trips = src.shape[1]
    width = w_basis.shape[1]
    tile = min(TILE, trips)
    row = pl.BlockSpec((1, tile), lambda i: (0, i))
    return pl.pallas_call(
        functools.partial(forward_kernel, groups, edges, width),
        grid=(trips // tile,),
        out_shape=[
            jax.ShapeDtypeStruct((width, edges), BF16),
            jax.ShapeDtypeStruct((width, trips), BF16),
        ],
        in_specs=[
            row,
            row,
            pl.BlockSpec((basis.shape[0], tile), lambda i: (0, i)),
            pl.BlockSpec(w_basis.shape, lambda i: (0, 0)),
            pl.BlockSpec(table.shape, lambda i: (0, 0)),
        ],
        out_specs=[
            pl.BlockSpec((width, edges), lambda i: (0, 0)),
            pl.BlockSpec((width, tile), lambda i: (0, i)),
        ],
        scratch_shapes=[pltpu.VMEM((edges // SUB * width, SUB), F32)],
        name="forward_triplets",
    )(src, tgt, basis, w_basis, table)


def backward_kernel(
    groups,
    edges,
    width,
    src_ref,
    tgt_ref,
    basis_ref,
    wb_ref,
    din_ref,
    dagg_ref,
    part_ref,
    bg_ref,
    acc,
    stack_ref,
):
    step = pl.program_id(0)
    subs = edges // SUB

    @pl.when(step == 0)
    def _():
        acc[...] = jnp.zeros_like(acc)
        bg_ref[...] = jnp.zeros_like(bg_ref)
        for h in range(subs):
            stack_ref[h * width : (h + 1) * width, :] = dagg_ref[:, h * SUB : (h + 1) * SUB]

    src = src_ref[...]
    tgt = tgt_ref[...]
    owner = src // edges
    high = tgt // SUB
    dagg_out = pick(
        dot(stack_ref[...], one_hot(SUB, tgt - high * SUB), NN), high, subs, width
    )
    dcoeff = (dagg_out * din_ref[...].astype(F32)).astype(BF16)
    bg_ref[...] += dot(basis_ref[...], dcoeff, NT)
    coeff = dot(wb_ref[...], basis_ref[...], TN)
    acc[...] += dot(
        place(dagg_out * coeff, owner, groups), one_hot(edges, src - owner * edges), NT
    )

    @pl.when(step == pl.num_programs(0) - 1)
    def _():
        part_ref[...] = acc[...].astype(BF16)


def backward_triplets(groups, edges, src, tgt, basis, w_basis, down_in, dagg):
    trips = src.shape[1]
    width = w_basis.shape[1]
    tile = min(TILE, trips)
    row = pl.BlockSpec((1, tile), lambda i: (0, i))
    return pl.pallas_call(
        functools.partial(backward_kernel, groups, edges, width),
        grid=(trips // tile,),
        out_shape=[
            jax.ShapeDtypeStruct((groups * width, edges), BF16),
            jax.ShapeDtypeStruct(w_basis.shape, F32),
        ],
        in_specs=[
            row,
            row,
            pl.BlockSpec((basis.shape[0], tile), lambda i: (0, i)),
            pl.BlockSpec(w_basis.shape, lambda i: (0, 0)),
            pl.BlockSpec((width, tile), lambda i: (0, i)),
            pl.BlockSpec(dagg.shape, lambda i: (0, 0)),
        ],
        out_specs=[
            pl.BlockSpec((groups * width, edges), lambda i: (0, 0)),
            pl.BlockSpec(w_basis.shape, lambda i: (0, 0)),
        ],
        scratch_shapes=[
            pltpu.VMEM((groups * width, edges), F32),
            pltpu.VMEM((edges // SUB * width, SUB), BF16),
        ],
        name="backward_triplets",
    )(src, tgt, basis, w_basis, down_in, dagg)


def on_device(
    edge_feats,
    cotangent,
    angle_basis,
    source_edge,
    target_edge,
    pair_weight,
    down_weight,
    basis_weight,
    up_weight,
    res_first,
    res_second,
):
    scale = math.sqrt(0.5)
    n = lax.axis_size("dp")
    groups = lax.axis_size("graph")
    w_pair, w_down, w_basis, w_up, w_first, w_second = [
        item.reshape(-1, item.shape[2])
        for item in gather_weights(
            n, (pair_weight, down_weight, basis_weight, up_weight, res_first, res_second)
        )
    ]
    edges = edge_feats.shape[0]
    width = w_down.shape[1]
    src = source_edge.reshape(1, -1)
    tgt = target_edge.reshape(1, -1)
    z_one = jnp.dot(edge_feats, w_pair, preferred_element_type=F32)
    hidden = jax.nn.silu(z_one).astype(BF16)
    down_t = jnp.einsum("ed,dk->ke", hidden, w_down, preferred_element_type=F32).astype(BF16)
    table = spread_down(groups, down_t).reshape(groups * width, edges)
    agg_t, down_in = forward_triplets(groups, edges, src, tgt, angle_basis, w_basis, table)
    z_two = jnp.einsum("ke,kd->ed", agg_t, w_up, preferred_element_type=F32)
    mixed = jax.nn.silu(z_two).astype(BF16)
    z_three = jnp.dot(mixed, w_first, preferred_element_type=F32)
    inner = jax.nn.silu(z_three).astype(BF16)
    z_four = jnp.dot(inner, w_second, preferred_element_type=F32)
    dz_four = (scale * cotangent.astype(F32) * silu_slope(z_four)).astype(BF16)
    dz_three = (
        jnp.einsum("ed,fd->ef", dz_four, w_second, preferred_element_type=F32) * silu_slope(z_three)
    ).astype(BF16)
    dmixed = scale * cotangent.astype(F32) + jnp.einsum(
        "ed,fd->ef", dz_three, w_first, preferred_element_type=F32
    )
    dz_two = (dmixed * silu_slope(z_two)).astype(BF16)
    dagg_t = jnp.einsum("kd,ed->ke", w_up, dz_two, preferred_element_type=F32).astype(BF16)
    partial, basis_local = backward_triplets(
        groups, edges, src, tgt, angle_basis, w_basis, down_in, dagg_t
    )
    ddown_t = collect_down(groups, partial.reshape(groups, width, edges))
    second_local = jnp.einsum("ed,ef->df", inner, dz_four, preferred_element_type=F32)
    first_local = jnp.einsum("ed,ef->df", mixed, dz_three, preferred_element_type=F32)
    up_local = jnp.einsum("ke,ed->kd", agg_t, dz_two, preferred_element_type=F32)
    down_local = jnp.einsum("ed,ke->dk", hidden, ddown_t, preferred_element_type=F32)
    dz_one = (
        jnp.einsum("ke,dk->ed", ddown_t, w_down, preferred_element_type=F32) * silu_slope(z_one)
    ).astype(BF16)
    pair_local = jnp.einsum("ed,ef->df", edge_feats, dz_one, preferred_element_type=F32)
    edge_grad = jnp.einsum("ef,df->ed", dz_one, w_pair, preferred_element_type=F32).astype(BF16)

    def large(item):
        rows, cols = item.shape
        return item.astype(BF16).reshape(n, groups, rows // (n * groups), cols)

    def small(item, kind):
        return item.astype(kind).reshape(n, item.shape[0] // n, item.shape[1])

    second_sum, first_sum, pair_sum, up_sum, down_sum, basis_sum = total_grads(
        n,
        groups,
        (
            large(second_local),
            large(first_local),
            large(pair_local),
            small(up_local, BF16),
            small(down_local, BF16),
            small(basis_local, F32),
        ),
        (True, True, True, False, False, False),
    )
    return (
        edge_grad,
        pair_sum.reshape(-1, pair_sum.shape[2]),
        down_sum,
        basis_sum,
        up_sum,
        first_sum.reshape(-1, first_sum.shape[2]),
        second_sum.reshape(-1, second_sum.shape[2]),
    )


def solution(mesh):
    return jax.shard_map(
        on_device,
        mesh=mesh,
        in_specs=(
            P(("dp", "graph"), None),
            P(("dp", "graph"), None),
            P(None, ("dp", "graph")),
            P(("dp", "graph")),
            P(("dp", "graph")),
            P("dp", None),
            P("dp", None),
            P("dp", None),
            P("dp", None),
            P("dp", None),
            P("dp", None),
        ),
        out_specs=(
            P(("dp", "graph"), None),
            P("dp", None),
            P("dp", None),
            P("dp", None),
            P("dp", None),
            P("dp", None),
            P("dp", None),
        ),
        check_vma=False,
    )
```

time: 482 us -> 133 us (0.28)
  waiting for transfers between devices: 145 us -> 0 us
  blocking collectives: 99.5 us -> 0 us
  Pallas kernels: 0 us -> 96.5 us
  other arithmetic: 96.3 us -> 0 us
  local copies, waits for them, and re-layouts: 102 us -> 11 us
  between operations: 14.7 us -> 0.79 us
    all_gather x7 -> x0, blocking collectives: 99.5 us -> none  [the longest x1 16.1 us: on_device(): lax.all_gather(res_second, 'dp', axis=0, tiled=True)]
    pallas_call x0 -> x6, Pallas kernels: none -> 96.5 us  [the longest x1 26.2 us: total_grads(): pl.pallas_call(functools.partial(total_kernel, n, groups, kinds), out_sha...]
    scatter-add x2 -> x0, other arithmetic: 90.5 us -> none  [the longest x1 45.9 us: on_device(): jnp.zeros((width_trip, group_cols), f32).at[:, source_edge]]
    unnamed x4 -> x0, waiting for transfers between devices: 80.9 us -> none
    gather x4 -> x0, local copies, waits for them, and re-layouts: 63.7 us -> none  [the longest x2 32 us: on_device(): down_in = jnp.take(group_down, source_edge, axis=1).astype(f32)]
    psum x1 -> x0, waiting for transfers between devices: 43.6 us -> none  [on_device(): shares = lax.psum(rows_sum, 'graph')]
    reduce_scatter x1 -> x0, waiting for transfers between devices: 20.7 us -> none  [on_device(): lax.psum_scatter(partial_down, 'graph', scatter_dimension=1, tiled=True)]
    reshape x13 -> x0, local copies, waits for them, and re-layouts: 13.3 us -> none  [the longest x6 5.16 us: on_device(): item.reshape(data_count, -1)]
  transfers between devices with their start and end apart: 3 -> 0, of which waited for: 3 -> 0; matrix products, arithmetic and copies ran while one was open for 3% -> 0% of each run, Pallas kernels for 0% -> 0%
where the time goes in v1:
time: 133 us
  Pallas kernels  96.5 us (73%)
  matrix products  24.3 us (18%)
  local copies, waits for them, and re-layouts  11 us (8%)
    pallas_call x1, Pallas kernels, total_grads(): pl.pallas_call(functools.partial(total_kernel, n, groups, kinds), out_sha...  26.2 us
    pallas_call x1, Pallas kernels, gather_weights(): pl.pallas_call(functools.partial(gather_kernel, n, count), out_shape=[jax...  24.1 us
    pallas_call x1, Pallas kernels, forward_triplets(): pl.pallas_call(functools.partial(forward_kernel, groups, edges, width), g...  12.5 us
    pallas_call x1, Pallas kernels, backward_triplets(): pl.pallas_call(functools.partial(backward_kernel, groups, edges, width),...  11.4 us
    pallas_call x1, Pallas kernels, spread_down(): pl.pallas_call(functools.partial(spread_kernel, groups), out_shape=jax.Sh...  11.4 us
    pallas_call x1, Pallas kernels, collect_down(): pl.pallas_call(functools.partial(collect_kernel, groups), out_shape=jax.S...  11 us
    unnamed x25, local copies, waits for them, and re-layouts  10.2 us
    dot_general x1, matrix products, on_device(): jnp.einsum('ke,dk->ed', ddown_t, w_down, preferred_element_type=F32)  3.5 us

profile of v1, /device:TPU:0, one launch (start us, length us, event | category | flops | bytes accessed | tf_op | source)
XLA Modules:
  0.0 132.6 jit_solution(10632896877565274157)
XLA Ops:
  0.6 0.0 copy-start
  0.6 1.6 %copy.18 = bf16[1024,512]{0,1:T(8,128)(2,1)S(1)} copy(bf16[1024,512]{1,0:T(8,128)(2,1)} %param.12) | data formatting | bytes 2097152 | tf_op args[1]
  2.2 24.1 %gather_weights.1 = (bf16[8,64,512]{2,1,0:T(8,128)(2,1)}, bf16[8,64,64]{2,1,0:T(8,128)(2,1)}, bf16[8,2,64]{2,1,0:T(2,128)(2,1)}, bf16[8,8,512]{2,1,0:T(8,128)(2,...) custom-call(bf16[64,512]{1,0:T(8,128)(2,1)} %refs_0_.1, bf16[64,64]{1,0:T(8,128)(2,1)} %refs_1_.1, ...), custom_call_target="tpu_custom_call" | custom-call | tf_op jit(solution)/shard_map/gather_weights/pallas_call | solution.py:122
  26.3 0.0 copy-done
  26.4 0.0 copy-start.2
  26.4 3.4 %fusion.3 = (bf16[1024,512]{0,1:T(8,128)(2,1)S(1)}, f32[512,1024]{1,0:T(8,128)}) fusion(bf16[512,512]{1,0:T(8,128)(2,1)} %bitcast.98, bf16[1024,512]{1,0:T(8,128)(2,1)S(1)} %copy-done), kind=kOutput, calls=%fused_computation.6 | convolution fusion | flops 539492352 | bytes 4718592 | tf_op jit(solution)/shard_map/dot_general | solution.py:566
  29.8 0.0 copy-start.4
  29.8 0.0 copy-done.2
  29.8 1.0 convolution_convert_fusion.5.in_ref
  30.7 11.4 %spread_down.1 = bf16[4,64,1024]{2,1,0:T(8,128)(2,1)} custom-call(bf16[64,1024]{1,0:T(8,128)(2,1)} %convolution_convert_fusion.5.in_ref), custom_call_target="tpu_custom_call" | custom-call | tf_op jit(solution)/shard_map/spread_down/pallas_call | solution.py:161
  42.1 12.5 %forward_triplets.1 = (bf16[64,1024]{1,0:T(8,128)(2,1)}, bf16[64,8192]{1,0:T(8,128)(2,1)}) custom-call(s32[1,8192]{1,0:T(1,128)} %bitcast.91, s32[1,8192]{1,0:T(1,128)} %bitcast.93, bf16[16,8192]{1,0:T(8,128)(2,1)} %basis_ref.3, bf16[16,64]{1,0:T(8,128)(2,1)} %bitcast.95, bf16[256,1024]{1,0:T(8,128)(2,1)} %bitcast.80), custom_call_target="tpu_custom_call" | custom-call | tf_op jit(solution)/shard_map/forward_triplets/pallas_call | solution.py:441
  54.6 0.0 copy-done.4
  54.6 0.0 copy-start.6
  54.6 1.7 %multiply_convert_fusion.4 = (bf16[1024,512]{0,1:T(8,128)(2,1)S(1)}, f32[1024,512]{0,1:T(8,128)S(1)}) fusion(bf16[64,1024]{1,0:T(8,128)(2,1)} %get-tuple-element.28, bf16[8,8,512]{2,1,0:T(8,128)(2,1)S(1)} %copy-done.4), kind=kOutput, calls=%fused_computation.16 | convolution fusion | flops 69730304 | bytes 3342336 | tf_op jit(solution)/shard_map/ke,kd->ed/dot_general | solution.py:571
  56.3 0.0 copy-done.6
  56.3 0.0 copy-start.7
  56.3 1.0 multiply_convert_fusion.3
  57.4 0.0 copy-done.7
  57.4 1.3 multiply_convert_fusion.2
  58.7 1.1 multiply_convert_fusion.1
  59.8 1.2 multiply_convert_fusion
  61.0 1.5 %convolution_convert_fusion.2 = bf16[512,512]{1,0:T(8,128)(2,1)} fusion(bf16[1024,512]{0,1:T(8,128)(2,1)S(1)} %get-tuple-element.41, bf16[1024,512]{0,1:T(8,128)(2,1)S(1)} %multiply_convert_fusion.1), kind=kOutput, calls=%fused_computation.21 | convolution fusion | flops 537133056 | bytes 2621440 | tf_op jit(solution)/shard_map/ed,ef->df/dot_general | solution.py:590
  62.5 0.0 copy-start.3
  62.5 1.6 %convolution_convert_fusion.3 = bf16[512,512]{1,0:T(8,128)(2,1)} fusion(bf16[1024,512]{0,1:T(8,128)(2,1)S(1)} %get-tuple-element.43, bf16[1024,512]{0,1:T(8,128)(2,1)S(1)} %multiply_convert_fusion.2), kind=kOutput, calls=%fused_computation.22 | convolution fusion | flops 537133056 | bytes 2621440 | tf_op jit(solution)/shard_map/ed,ef->df/dot_general | solution.py:589
  64.1 0.0 copy-done.3
  64.1 1.1 fusion.8.refs_3_
  65.2 1.0 convolution_convert_fusion.4.dagg_ref
  66.1 11.4 %backward_triplets.1 = (bf16[256,1024]{1,0:T(8,128)(2,1)}, f32[16,64]{1,0:T(8,128)}) custom-call(s32[1,8192]{1,0:T(1,128)} %bitcast.92, s32[1,8192]{1,0:T(1,128)} %bitcast.94, bf16[16,8192]{1,0:T(8,128)(2,1)} %basis_ref.3, bf16[16,64]{1,0:T(8,128)(2,1)} %bitcast.96, bf16[64,8192]{1,0:T(8,128)(2,1)} %get-tuple-element.26.din_ref, ...), custom_call_target="tpu_custom_call" | custom-call | tf_op jit(solution)/shard_map/backward_triplets/pallas_call | solution.py:513
  77.5 11.0 %collect_down.1 = bf16[64,1024]{1,0:T(8,128)(2,1)} custom-call(bf16[4,64,1024]{2,1,0:T(8,128)(2,1)} %bitcast.84), custom_call_target="tpu_custom_call" | custom-call | tf_op jit(solution)/shard_map/collect_down/pallas_call | solution.py:191
  88.5 0.0 copy-start.1
  88.5 3.5 %fusion.7 = bf16[1024,512]{0,1:T(8,128)(2,1)} fusion(f32[512,1024]{1,0:T(8,128)} %get-tuple-element.40, bf16[512,64]{1,0:T(8,128)(2,1)S(1)} %bitcast.87, bf16[64,1024]{1,0:T(8,128)(2,1)} %collect_down.1), kind=kOutput, calls=%fused_computation.10 | convolution fusion | flops 71827456 | bytes 3342336 | tf_op jit(solution)/shard_map/ke,dk->ed/dot_general | solution.py:594
  92.0 0.0 copy-done.1
  92.1 0.4 convolution_convert_fusion.6
  92.5 0.0 copy-start.5
  92.5 0.0 copy-start.8
  92.5 0.8 copy.30
  93.3 2.8 %convolution_convert_fusion.1 = bf16[512,512]{0,1:T(8,128)(2,1)} fusion(bf16[1024,512]{0,1:T(8,128)(2,1)} %fusion.7, bf16[1024,512]{1,0:T(8,128)(2,1)S(1)} %copy-done), kind=kOutput, calls=%fused_computation.20 | convolution fusion | flops 537133056 | bytes 2621440 | tf_op jit(solution)/shard_map/ed,ef->df/dot_general | solution.py:596
  96.0 0.0 copy-done.5
  96.1 0.0 copy-done.8
  96.1 1.7 %convolution_convert_fusion = bf16[1024,512]{1,0:T(8,128)(2,1)} fusion(bf16[1024,512]{0,1:T(8,128)(2,1)S(1)} %copy-done.8, bf16[512,512]{1,0:T(8,128)(2,1)S(1)} %bitcast.99), kind=kOutput, calls=%fused_computation.19 | convolution fusion | flops 537395200 | bytes 2621440 | tf_op jit(solution)/shard_map/ef,df->ed/dot_general | solution.py:597
  97.8 26.2 %total_grads.1 = (f32[4,16,512]{2,1,0:T(8,128)}, f32[4,16,512]{2,1,0:T(8,128)}, f32[4,16,512]{2,1,0:T(8,128)}, f32[8,512]{1,0:T(8,128)}, f32[64,64]{1,0:T(8,128)}, /*index=5*/f32[2,64]{1,0:T(2,128)}) custom-call(bf16[8,4,16,512]{3,2,1,0:T(8,128)(2,1)} %bitcast.82, bf16[8,4,16,512]{3,2,1,0:T(8,128)(2,1)} %bitcast.81, bf16[8,4,16,512]{3,2,1,0:T(8,128)(2,1)} %bitcast.83, ...), custom_call_target="tpu_custom_call" | custom-call | tf_op jit(solution)/shard_map/total_grads/pallas_call | solution.py:372
  124.0 1.6 %copy.43 = f32[64,512]{1,0:T(8,128)} copy(f32[64,512]{1,0:T(8,128)} %bitcast.90) | data formatting | bytes 262144
  125.6 1.4 %copy.44 = f32[64,64]{1,0:T(8,128)} copy(f32[64,64]{1,0:T(8,128)} %get-tuple-element.54) | data formatting | bytes 32768
  126.9 1.2 copy.45
  128.2 1.3 copy.46
  129.5 1.6 %copy.47 = f32[64,512]{1,0:T(8,128)} copy(f32[64,512]{1,0:T(8,128)} %bitcast.89) | data formatting | bytes 262144
  131.1 1.6 %copy.48 = f32[64,512]{1,0:T(8,128)} copy(f32[64,512]{1,0:T(8,128)} %bitcast.88) | data formatting | bytes 262144
Async XLA Ops:
  0.6 25.7 %copy-start = (bf16[1024,512]{1,0:T(8,128)(2,1)S(1)}, bf16[1024,512]{1,0:T(8,128)(2,1)}, u32[]{:S(2)}) copy-start(bf16[1024,512]{1,0:T(8,128)(2,1)} %param.11) | copy-start | bytes 3145732
  26.4 3.4 %copy-start.2 = (bf16[8,64,64]{2,1,0:T(8,128)(2,1)S(1)}, bf16[8,64,64]{2,1,0:T(8,128)(2,1)}, u32[]{:S(2)}) copy-start(bf16[8,64,64]{2,1,0:T(8,128)(2,1)} %get-tuple-element.24) | copy-start | bytes 196612
  29.8 24.8 %copy-start.4 = (bf16[8,8,512]{2,1,0:T(8,128)(2,1)S(1)}, bf16[8,8,512]{2,1,0:T(8,128)(2,1)}, u32[]{:S(2)}) copy-start(bf16[8,8,512]{2,1,0:T(8,128)(2,1)} %get-tuple-element.27) | copy-start | bytes 196612
  54.6 1.7 %copy-start.6 = (bf16[8,64,512]{2,1,0:T(8,128)(2,1)S(1)}, bf16[8,64,512]{2,1,0:T(8,128)(2,1)}, u32[]{:S(2)}) copy-start(bf16[8,64,512]{2,1,0:T(8,128)(2,1)} %get-tuple-element.29) | copy-start | bytes 1572868
  56.3 1.1 copy-start.7
  62.5 1.6 %copy-start.3 = (bf16[64,1024]{1,0:T(8,128)(2,1)S(1)}, bf16[64,1024]{1,0:T(8,128)(2,1)}, u32[]{:S(2)}) copy-start(bf16[64,1024]{1,0:T(8,128)(2,1)} %get-tuple-element.28) | copy-start | bytes 393220
  88.5 3.5 %copy-start.1 = (bf16[64,1024]{1,0:T(8,128)(2,1)S(1)}, bf16[64,1024]{1,0:T(8,128)(2,1)}, u32[]{:S(2)}) copy-start(bf16[64,1024]{1,0:T(8,128)(2,1)} %collect_down.1) | copy-start | bytes 393220
  92.5 3.6 %copy-start.5 = (bf16[8,64,512]{2,1,0:T(8,128)(2,1)S(1)}, bf16[8,64,512]{2,1,0:T(8,128)(2,1)}, u32[]{:S(2)}) copy-start(bf16[8,64,512]{2,1,0:T(8,128)(2,1)} %get-tuple-element.25) | copy-start | bytes 1572868
  92.5 3.6 %copy-start.8 = (bf16[1024,512]{0,1:T(8,128)(2,1)S(1)}, bf16[1024,512]{0,1:T(8,128)(2,1)}, u32[]{:S(2)}) copy-start(bf16[1024,512]{0,1:T(8,128)(2,1)} %fusion.7) | copy-start | bytes 3145732

commit v2 on v1

v2 whole, which is shorter than its diff:
```python
import functools
import math

import jax
import jax.numpy as jnp
from jax import lax
from jax.experimental import pallas as pl
from jax.experimental.pallas import tpu as pltpu
from jax.sharding import PartitionSpec as P

MESH = pl.DeviceIdType.MESH
F32 = jnp.float32
BF16 = jnp.bfloat16
VM = pl.BlockSpec(memory_space=pltpu.VMEM)
SUB = 256
TILE = 1024


def remote(src, dst, send, recv, target):
    return pltpu.make_async_remote_copy(
        src_ref=src,
        dst_ref=dst,
        send_sem=send,
        recv_sem=recv,
        device_id=target,
        device_id_type=MESH,
    )


def silu_slope(value):
    sig = jax.nn.sigmoid(value)
    return sig * (1.0 + value * (1.0 - sig))


def greet(targets, waits):
    barrier = pltpu.get_barrier_semaphore()
    for target in targets:
        pl.semaphore_signal(barrier, inc=1, device_id=target, device_id_type=MESH)
    pl.semaphore_wait(barrier, waits)


def graph_peers(groups):
    me = lax.axis_index("graph")
    return [{"graph": (me + k) % groups} for k in range(1, groups)]


def chip_peers(n):
    half = n // 2
    dp = lax.axis_index("dp")
    return [{"dp": (dp // 2 + k) % half * 2 + dp % 2} for k in range(1, half)]


def core_peer():
    dp = lax.axis_index("dp")
    return [{"dp": dp + 1 - 2 * (dp % 2)}]


def gather_steps(n, ins, outs, send, recv):
    count = len(ins)
    half = n // 2
    dp = lax.axis_index("dp")
    pos = dp // 2
    core = dp % 2
    partner = dp + 1 - 2 * core
    has_up = pos < half - 1
    has_down = pos > 0

    def copy(w, src, shard, way, target):
        return remote(
            src, outs[w].at[shard], send.at[shard, way, w], recv.at[shard, w], {"dp": target}
        )

    for w in range(count):

        @pl.when(has_up)
        def _():
            copy(w, ins[w], dp, 0, dp + 2).start()

        @pl.when(has_down)
        def _():
            copy(w, ins[w], dp, 1, dp - 2).start()

        copy(w, ins[w], dp, 2, partner).start()
    for w in range(count):
        outs[w][dp] = ins[w][...]
    yield
    for k in range(1, half):
        for w in range(count):

            @pl.when(pos >= k)
            def _():
                shard = dp - 2 * k
                block = outs[w].at[shard]
                copy(w, block, shard, 2, partner).wait_recv()

                @pl.when(has_up)
                def _():
                    copy(w, block, shard, 0, dp + 2).start()

                copy(w, block, shard, 2, partner).start()

            @pl.when(pos + k < half)
            def _():
                shard = dp + 2 * k
                block = outs[w].at[shard]
                copy(w, block, shard, 2, partner).wait_recv()

                @pl.when(has_down)
                def _():
                    copy(w, block, shard, 1, dp - 2).start()

                copy(w, block, shard, 2, partner).start()

        yield
    for w in range(count):
        for q in range(half):
            shard = 2 * q + 1 - core
            copy(w, outs[w].at[shard], shard, 2, partner).wait_recv()
            mine = 2 * q + core
            copy(w, outs[w].at[mine], mine, 2, partner).wait_send()

            @pl.when(jnp.logical_and(pos >= q, has_up))
            def _():
                copy(w, outs[w].at[mine], mine, 0, dp + 2).wait_send()

            @pl.when(jnp.logical_and(pos <= q, has_down))
            def _():
                copy(w, outs[w].at[mine], mine, 1, dp - 2).wait_send()


def gather_kernel(n, count, *refs):
    greet(chip_peers(n) + core_peer(), n // 2)
    for _ in gather_steps(n, refs[:count], refs[count : 2 * count], *refs[2 * count :]):
        pass


def gather_sems(n, count):
    return [pltpu.SemaphoreType.DMA((n, 3, count)), pltpu.SemaphoreType.DMA((n, count))]


def gathered(n, weights):
    return [jax.ShapeDtypeStruct((n,) + w.shape, w.dtype) for w in weights]


def gather_weights(n, weights):
    count = len(weights)
    return pl.pallas_call(
        functools.partial(gather_kernel, n, count),
        out_shape=gathered(n, weights),
        in_specs=[VM] * count,
        out_specs=[VM] * count,
        scratch_shapes=gather_sems(n, count),
        compiler_params=pltpu.CompilerParams(collective_id=0, has_side_effects=True),
        name="gather_weights",
    )(*weights)


def total_steps(n, groups, kinds, ins, outs, refs):
    count = len(kinds)
    scratch = []
    place_at = 0
    for large in kinds:
        size = 6 if large else 4
        scratch.append(refs[place_at : place_at + size])
        place_at += size
    a_send, a_recv, b_send, b_recv, c_send, c_recv, d_send, d_recv = refs[place_at:]
    half = n // 2
    dp = lax.axis_index("dp")
    me = lax.axis_index("graph")
    pos = dp // 2
    core = dp % 2
    partner = dp + 1 - 2 * core
    sent = []

    def send_all(copies):
        for cp in copies:
            cp.start()
        sent.extend(copies)
        return copies

    first = []
    for w in range(count):
        first.append(
            send_all(
                [
                    remote(
                        ins[w].at[2 * q + 1 - core],
                        scratch[w][0].at[q],
                        a_send.at[w, q],
                        a_recv.at[w, q],
                        {"dp": partner},
                    )
                    for q in range(half)
                ]
            )
        )
    yield
    second = []
    for w, large in enumerate(kinds):
        got, summed = scratch[w][0], scratch[w][1]
        for q in range(half):
            first[w][q].wait_recv()
            value = ins[w][2 * q + core].astype(F32) + got[q].astype(F32)
            if large:
                summed[:, q] = value.astype(summed.dtype)
            else:
                summed[q] = value.astype(summed.dtype)
        copies = []
        if large:
            copies = [
                remote(
                    summed.at[(me + k) % groups],
                    scratch[w][4].at[k],
                    b_send.at[w, k],
                    b_recv.at[w, k],
                    {"graph": (me + k) % groups},
                )
                for k in range(1, groups)
            ]
        second.append(send_all(copies))
    yield
    third = []
    for w, large in enumerate(kinds):
        part = scratch[w][1]
        if large:
            for cp in second[w]:
                cp.wait_recv()
            value = scratch[w][1][me].astype(F32)
            for k in range(1, groups):
                value = value + scratch[w][4][k].astype(F32)
            part = scratch[w][5]
            part[...] = value.astype(part.dtype)
        third.append(
            send_all(
                [
                    remote(
                        part.at[(pos + k) % half],
                        scratch[w][2].at[k],
                        c_send.at[w, k],
                        c_recv.at[w, k],
                        {"dp": (pos + k) % half * 2 + core},
                    )
                    for k in range(1, half)
                ]
            )
        )
    yield
    fourth = []
    for w, large in enumerate(kinds):
        part = scratch[w][5] if large else scratch[w][1]
        for cp in third[w]:
            cp.wait_recv()
        value = part[pos].astype(F32)
        for k in range(1, half):
            value = value + scratch[w][2][k].astype(F32)
        done = scratch[w][3]
        done[...] = value.astype(done.dtype)
        fourth.append(
            send_all(
                [
                    remote(
                        done,
                        outs[w].at[me],
                        d_send.at[w, k],
                        d_recv.at[w, k],
                        {"graph": (me + k) % groups},
                    )
                    for k in range(1, groups)
                ]
            )
        )
        outs[w][me] = value.astype(done.dtype)
    yield
    for copies in fourth:
        for cp in copies:
            cp.wait_recv()
    for cp in sent:
        cp.wait_send()


def total_parts(n, groups, grads, kinds):
    half = n // 2
    shapes, scratch = [], []
    for item, large in zip(grads, kinds):
        tail = item.shape[2:] if large else item.shape[1:]
        kind = item.dtype
        shapes.append(jax.ShapeDtypeStruct((groups,) + tail, kind))
        scratch.append(pltpu.VMEM((half,) + item.shape[1:], kind))
        scratch.append(
            pltpu.VMEM(((groups, half) + tail) if large else ((half,) + tail), kind)
        )
        scratch.append(pltpu.VMEM((half,) + tail, kind))
        scratch.append(pltpu.VMEM(tail, kind))
        if large:
            scratch.append(pltpu.VMEM((groups, half) + tail, kind))
            scratch.append(pltpu.VMEM((half,) + tail, kind))
    for length in (half, groups, half, groups):
        scratch += [pltpu.SemaphoreType.DMA((len(grads), length))] * 2
    return shapes, scratch


def greet_all(n, groups):
    greet(core_peer() + graph_peers(groups) + chip_peers(n), groups + n // 2 - 1)


def total_kernel(n, groups, kinds, *refs):
    count = len(kinds)
    greet_all(n, groups)
    for _ in total_steps(
        n, groups, kinds, refs[:count], refs[count : 2 * count], refs[2 * count :]
    ):
        pass


def total_grads(n, groups, grads, kinds):
    count = len(grads)
    shapes, scratch = total_parts(n, groups, grads, kinds)
    return pl.pallas_call(
        functools.partial(total_kernel, n, groups, kinds),
        out_shape=shapes,
        in_specs=[VM] * count,
        out_specs=[VM] * count,
        scratch_shapes=scratch,
        compiler_params=pltpu.CompilerParams(collective_id=3, has_side_effects=True),
        name="total_grads",
    )(*grads)


def write_kernel(kinds, *refs):
    for large, landed, out in zip(kinds, refs[: len(kinds)], refs[len(kinds) :]):
        groups, rows = landed.shape[0], landed.shape[1]
        if large:
            for g in range(groups):
                out[g * rows : (g + 1) * rows, :] = landed[g].astype(F32)
        else:
            value = landed[0].astype(F32)
            for g in range(1, groups):
                value = value + landed[g].astype(F32)
            out[...] = value


def write_grads(landed, kinds):
    return pl.pallas_call(
        functools.partial(write_kernel, kinds),
        out_shape=[
            jax.ShapeDtypeStruct(
                (item.shape[1] * (item.shape[0] if large else 1), item.shape[2]), F32
            )
            for item, large in zip(landed, kinds)
        ],
        in_specs=[VM] * len(kinds),
        out_specs=[VM] * len(kinds),
        name="write_grads",
    )(*landed)


def one_hot(size, row):
    spots = lax.broadcasted_iota(jnp.int32, (size, row.shape[1]), 0)
    return jnp.where(spots == row, 1.0, 0.0).astype(BF16)


def pick(stack, owner, groups, width):
    value = jnp.where(owner == 0, stack[:width], 0.0)
    for g in range(1, groups):
        value = value + jnp.where(owner == g, stack[g * width : (g + 1) * width], 0.0)
    return value


def place(value, owner, groups):
    return jnp.concatenate(
        [jnp.where(owner == g, value, 0.0).astype(BF16) for g in range(groups)], axis=0
    )


def dot(a, b, dims):
    return lax.dot_general(a, b, (dims, ((), ())), preferred_element_type=F32)


NN = ((1,), (0,))
NT = ((1,), (1,))
TN = ((0,), (0,))


def forward_kernel(
    n,
    groups,
    src_ref,
    tgt_ref,
    basis_ref,
    wb_ref,
    down_ref,
    up_ref,
    first_ref,
    second_ref,
    agg_ref,
    din_ref,
    up_out,
    first_out,
    second_out,
    acc,
    table,
    send,
    recv,
    w_send,
    w_recv,
):
    width, edges = down_ref.shape
    subs = edges // SUB
    trips = src_ref.shape[1]
    tile = min(TILE, trips)
    me = lax.axis_index("graph")
    greet(
        graph_peers(groups) + chip_peers(n) + core_peer(), groups - 1 + n // 2
    )
    copies = []
    for k in range(1, groups):
        cp = remote(
            down_ref, table.at[me], send.at[k], recv.at[k], {"graph": (me + k) % groups}
        )
        cp.start()
        copies.append(cp)
    steps = gather_steps(
        n,
        (up_ref, first_ref, second_ref),
        (up_out, first_out, second_out),
        w_send,
        w_recv,
    )
    table[me] = down_ref[...]
    acc[...] = jnp.zeros_like(acc)

    def work(i, carry):
        spot = pl.ds(pl.multiple_of(i * tile, tile), tile)
        src = src_ref[:, spot]
        tgt = tgt_ref[:, spot]
        basis = basis_ref[:, spot]
        owner = src // edges
        stack = dot(
            table[...].reshape(groups * width, edges), one_hot(edges, src - owner * edges), NN
        )
        down_in = pick(stack, owner, groups, width)
        din_ref[:, spot] = down_in.astype(BF16)
        coeff = dot(wb_ref[...], basis, TN)
        high = tgt // SUB
        acc[...] += dot(
            place(down_in * coeff, high, subs), one_hot(SUB, tgt - high * SUB), NT
        )
        return carry

    next(steps)
    for cp in copies:
        cp.wait()
    tiles = trips // tile
    count = n // 2 - 1
    for i in range(count):
        lax.fori_loop(tiles * i // (count + 1), tiles * (i + 1) // (count + 1), work, 0)
        next(steps)
    lax.fori_loop(tiles * count // (count + 1), tiles, work, 0)
    for h in range(subs):
        agg_ref[:, h * SUB : (h + 1) * SUB] = acc[h * width : (h + 1) * width, :].astype(BF16)
    for _ in steps:
        pass


def forward_triplets(n, groups, src, tgt, basis, w_basis, down, weights):
    trips = src.shape[1]
    width, edges = down.shape
    return pl.pallas_call(
        functools.partial(forward_kernel, n, groups),
        out_shape=[
            jax.ShapeDtypeStruct((width, edges), BF16),
            jax.ShapeDtypeStruct((width, trips), BF16),
        ]
        + gathered(n, weights),
        in_specs=[VM] * 8,
        out_specs=[VM] * 5,
        scratch_shapes=[
            pltpu.VMEM((edges // SUB * width, SUB), F32),
            pltpu.VMEM((groups, width, edges), BF16),
        ]
        + [pltpu.SemaphoreType.DMA((groups,))] * 2
        + gather_sems(n, len(weights)),
        compiler_params=pltpu.CompilerParams(collective_id=1, has_side_effects=True),
        name="forward_triplets",
    )(src, tgt, basis, w_basis, down, *weights)


def backward_kernel(n, groups, kinds, *refs):
    src_ref, tgt_ref, basis_ref, wb_ref, din_ref, dagg_ref = refs[:6]
    count = len(kinds)
    ins = refs[6 : 6 + count]
    ddown_ref, bg_ref = refs[6 + count : 8 + count]
    outs = refs[8 + count : 8 + 2 * count]
    acc, stack_ref, part, landed, send, recv = refs[8 + 2 * count : 14 + 2 * count]
    rest = refs[14 + 2 * count :]
    width, edges = dagg_ref.shape
    subs = edges // SUB
    trips = src_ref.shape[1]
    tile = min(TILE, trips)
    me = lax.axis_index("graph")
    greet_all(n, groups)
    steps = total_steps(n, groups, kinds, ins, outs, rest)
    acc[...] = jnp.zeros_like(acc)
    bg_ref[...] = jnp.zeros_like(bg_ref)
    for h in range(subs):
        stack_ref[h * width : (h + 1) * width, :] = dagg_ref[:, h * SUB : (h + 1) * SUB]

    def work(i, carry):
        spot = pl.ds(pl.multiple_of(i * tile, tile), tile)
        src = src_ref[:, spot]
        tgt = tgt_ref[:, spot]
        basis = basis_ref[:, spot]
        owner = src // edges
        high = tgt // SUB
        dagg_out = pick(
            dot(stack_ref[...], one_hot(SUB, tgt - high * SUB), NN), high, subs, width
        )
        dcoeff = (dagg_out * din_ref[:, spot].astype(F32)).astype(BF16)
        bg_ref[...] += dot(basis, dcoeff, NT)
        coeff = dot(wb_ref[...], basis, TN)
        acc[...] += dot(
            place(dagg_out * coeff, owner, groups), one_hot(edges, src - owner * edges), NT
        )
        return carry

    tiles = trips // tile
    for i in range(4):
        next(steps)
        lax.fori_loop(tiles * i // 4, tiles * (i + 1) // 4, work, 0)
    for g in range(groups):
        part[g] = acc[g * width : (g + 1) * width, :].astype(BF16)
    copies = []
    for k in range(1, groups):
        peer = (me + k) % groups
        cp = remote(part.at[peer], landed.at[k], send.at[k], recv.at[k], {"graph": peer})
        cp.start()
        copies.append(cp)
    for _ in steps:
        pass
    for cp in copies:
        cp.wait()
    total = part[me].astype(F32)
    for k in range(1, groups):
        total = total + landed[k].astype(F32)
    ddown_ref[...] = total.astype(BF16)


def backward_triplets(n, groups, src, tgt, basis, w_basis, down_in, dagg, grads, kinds):
    width, edges = dagg.shape
    shapes, scratch = total_parts(n, groups, grads, kinds)
    return pl.pallas_call(
        functools.partial(backward_kernel, n, groups, kinds),
        out_shape=[
            jax.ShapeDtypeStruct((width, edges), BF16),
            jax.ShapeDtypeStruct(w_basis.shape, F32),
        ]
        + shapes,
        in_specs=[VM] * (6 + len(grads)),
        out_specs=[VM] * (2 + len(grads)),
        scratch_shapes=[
            pltpu.VMEM((groups * width, edges), F32),
            pltpu.VMEM((edges // SUB * width, SUB), BF16),
            pltpu.VMEM((groups, width, edges), BF16),
            pltpu.VMEM((groups, width, edges), BF16),
        ]
        + [pltpu.SemaphoreType.DMA((groups,))] * 2
        + scratch,
        compiler_params=pltpu.CompilerParams(collective_id=2, has_side_effects=True),
        name="backward_triplets",
    )(src, tgt, basis, w_basis, down_in, dagg, *grads)


def on_device(
    edge_feats,
    cotangent,
    angle_basis,
    source_edge,
    target_edge,
    pair_weight,
    down_weight,
    basis_weight,
    up_weight,
    res_first,
    res_second,
):
    scale = math.sqrt(0.5)
    n = lax.axis_size("dp")
    groups = lax.axis_size("graph")
    def whole(item):
        return item.reshape(-1, item.shape[2])

    def large(item):
        rows, cols = item.shape
        return item.astype(BF16).reshape(n, groups, rows // (n * groups), cols)

    def small(item, kind):
        return item.astype(kind).reshape(n, item.shape[0] // n, item.shape[1])

    w_pair, w_down, w_basis = map(
        whole, gather_weights(n, (pair_weight, down_weight, basis_weight))
    )
    src = source_edge.reshape(1, -1)
    tgt = target_edge.reshape(1, -1)
    z_one = jnp.dot(edge_feats, w_pair, preferred_element_type=F32)
    hidden = jax.nn.silu(z_one).astype(BF16)
    down_t = jnp.einsum("ed,dk->ke", hidden, w_down, preferred_element_type=F32).astype(BF16)
    agg_t, down_in, w_up, w_first, w_second = forward_triplets(
        n,
        groups,
        src,
        tgt,
        angle_basis,
        w_basis,
        down_t,
        (up_weight, res_first, res_second),
    )
    w_up, w_first, w_second = whole(w_up), whole(w_first), whole(w_second)
    z_two = jnp.einsum("ke,kd->ed", agg_t, w_up, preferred_element_type=F32)
    mixed = jax.nn.silu(z_two).astype(BF16)
    z_three = jnp.dot(mixed, w_first, preferred_element_type=F32)
    inner = jax.nn.silu(z_three).astype(BF16)
    z_four = jnp.dot(inner, w_second, preferred_element_type=F32)
    dz_four = (scale * cotangent.astype(F32) * silu_slope(z_four)).astype(BF16)
    dz_three = (
        jnp.einsum("ed,fd->ef", dz_four, w_second, preferred_element_type=F32) * silu_slope(z_three)
    ).astype(BF16)
    dmixed = scale * cotangent.astype(F32) + jnp.einsum(
        "ed,fd->ef", dz_three, w_first, preferred_element_type=F32
    )
    dz_two = (dmixed * silu_slope(z_two)).astype(BF16)
    dagg_t = jnp.einsum("kd,ed->ke", w_up, dz_two, preferred_element_type=F32).astype(BF16)
    second_local = jnp.einsum("ed,ef->df", inner, dz_four, preferred_element_type=F32)
    first_local = jnp.einsum("ed,ef->df", mixed, dz_three, preferred_element_type=F32)
    up_local = jnp.einsum("ke,ed->kd", agg_t, dz_two, preferred_element_type=F32)
    ddown_t, basis_local, second_land, first_land, up_land = backward_triplets(
        n,
        groups,
        src,
        tgt,
        angle_basis,
        w_basis,
        down_in,
        dagg_t,
        (large(second_local), large(first_local), small(up_local, BF16)),
        (True, True, False),
    )
    down_local = jnp.einsum("ed,ke->dk", hidden, ddown_t, preferred_element_type=F32)
    dz_one = (
        jnp.einsum("ke,dk->ed", ddown_t, w_down, preferred_element_type=F32) * silu_slope(z_one)
    ).astype(BF16)
    pair_local = jnp.einsum("ed,ef->df", edge_feats, dz_one, preferred_element_type=F32)
    edge_grad = jnp.einsum("ef,df->ed", dz_one, w_pair, preferred_element_type=F32).astype(BF16)

    pair_land, down_land, basis_land = total_grads(
        n,
        groups,
        (large(pair_local), small(down_local, BF16), small(basis_local, F32)),
        (True, False, False),
    )
    return (
        edge_grad,
        *write_grads(
            (pair_land, down_land, basis_land, up_land, first_land, second_land),
            (True, False, False, False, True, True),
        ),
    )


def solution(mesh):
    return jax.shard_map(
        on_device,
        mesh=mesh,
        in_specs=(
            P(("dp", "graph"), None),
            P(("dp", "graph"), None),
            P(None, ("dp", "graph")),
            P(("dp", "graph")),
            P(("dp", "graph")),
            P("dp", None),
            P("dp", None),
            P("dp", None),
            P("dp", None),
            P("dp", None),
            P("dp", None),
        ),
        out_specs=(
            P(("dp", "graph"), None),
            P("dp", None),
            P("dp", None),
            P("dp", None),
            P("dp", None),
            P("dp", None),
            P("dp", None),
        ),
        check_vma=False,
    )
```

time: 133 us -> 118 us (0.89)
  local copies, waits for them, and re-layouts: 11 us -> 2.29 us
  Pallas kernels: 96.5 us -> 92.1 us
  matrix products: 24.3 us -> 22.1 us
    unnamed x25 -> x17, local copies, waits for them, and re-layouts: 10.2 us -> 1.53 us
    pallas_call x1, Pallas kernels: 26.2 us -> 18.3 us  [total_grads(): pl.pallas_call(functools.partial(total_kernel, n, groups, kinds), out_sha...]
    pallas_call x5 -> x4, Pallas kernels: 70.3 us -> 73.8 us  [the longest x1 27.7 us: backward_triplets(): pl.pallas_call(functools.partial(backward_kernel, n, groups, kinds), out_...]
where the time goes in v2:
time: 118 us; the launch traced here: 117 us
  Pallas kernels  92.1 us (78%)
  matrix products  22.1 us (19%)
  local copies, waits for them, and re-layouts  2.29 us (2%)
    pallas_call x1, Pallas kernels, backward_triplets(): pl.pallas_call(functools.partial(backward_kernel, n, groups, kinds), out_...  27.7 us
    pallas_call x1, Pallas kernels, forward_triplets(): pl.pallas_call(functools.partial(forward_kernel, n, groups), out_shape=[j...  26.2 us
    pallas_call x1, Pallas kernels, total_grads(): pl.pallas_call(functools.partial(total_kernel, n, groups, kinds), out_sha...  18.3 us
    pallas_call x1, Pallas kernels, gather_weights(): pl.pallas_call(functools.partial(gather_kernel, n, count), out_shape=gath...  18.2 us
    dot_general x1, matrix products, on_device(): z_one = jnp.dot(edge_feats, w_pair, preferred_element_type=F32)  3.39 us
    dot_general x1, matrix products, on_device(): jnp.einsum('ke,dk->ed', ddown_t, w_down, preferred_element_type=F32)  2.53 us

profile of v2, /device:TPU:0, one launch (start us, length us, event | category | flops | bytes accessed | tf_op | source)
XLA Modules:
  0.0 117.2 jit_solution(17224282801248563177)
XLA Ops:
  0.6 0.0 copy-start
  0.6 18.2 %gather_weights.1 = (bf16[8,64,512]{2,1,0:T(8,128)(2,1)}, bf16[8,64,64]{2,1,0:T(8,128)(2,1)}, bf16[8,2,64]{2,1,0:T(2,128)(2,1)}) custom-call(bf16[64,512]{1,0:T(8,128)(2,1)} %refs_0_.1, bf16[64,64]{1,0:T(8,128)(2,1)} %refs_1_.1, bf16[2,64]{1,0:T(2,128)(2,1)} %refs_2_.2), custom_call_target="tpu_custom_call" | custom-call | tf_op jit(solution)/shard_map/gather_weights/pallas_call | solution.py:147
  18.8 1.5 %copy.18 = bf16[1024,512]{0,1:T(8,128)(2,1)S(1)} copy(bf16[1024,512]{1,0:T(8,128)(2,1)} %param.12) | data formatting | bytes 2097152 | tf_op args[1]
  20.3 0.0 copy-done
  20.3 0.0 copy-start.1
  20.3 3.4 %fusion.3 = (bf16[1024,512]{0,1:T(8,128)(2,1)S(1)}, f32[512,1024]{1,0:T(8,128)}) fusion(bf16[512,512]{1,0:T(8,128)(2,1)} %bitcast.88, bf16[1024,512]{1,0:T(8,128)(2,1)S(1)} %copy-done), kind=kOutput, calls=%fused_computation.6 | convolution fusion | flops 539492352 | bytes 4718592 | tf_op jit(solution)/shard_map/dot_general | solution.py:604
  23.7 0.0 copy-done.1
  23.7 1.0 convolution_convert_fusion.5.down_ref
  24.7 26.2 %forward_triplets.1 = (bf16[64,1024]{1,0:T(8,128)(2,1)}, bf16[64,8192]{1,0:T(8,128)(2,1)}, bf16[8,8,512]{2,1,0:T(8,128)(2,1)}, bf16[8,64,512]{2,1,0:T(8,128)(2,1)}, bf16[8,64,512]{2,1,0:T(8,128)(2,1)}) custom-call(s32[1,8192]{1,0:T(1,128)} %bitcast.79, s32[1,8192]{1,0:T(1,128)} %bitcast.81, bf16[16,8192]{1,0:T(8,128)(2,1)} %refs_2_.3, ...), custom_call_target="tpu_custom_call" | custom-call | tf_op jit(solution)/shard_map/forward_triplets/pallas_call | solution.py:468
  50.9 0.0 copy-start.6
  50.9 1.7 %multiply_convert_fusion.4 = (bf16[1024,512]{0,1:T(8,128)(2,1)S(1)}, f32[1024,512]{0,1:T(8,128)S(1)}) fusion(bf16[64,1024]{1,0:T(8,128)(2,1)} %get-tuple-element.34, bf16[8,8,512]{2,1,0:T(8,128)(2,1)} %get-tuple-element.33), kind=kOutput, calls=%fused_computation.16 | convolution fusion | flops 69730304 | bytes 3342336 | tf_op jit(solution)/shard_map/ke,kd->ed/dot_general | solution.py:618
  52.6 0.0 copy-done.6
  52.6 0.0 copy-start.7
  52.6 1.0 multiply_convert_fusion.3
  53.7 0.0 copy-done.7
  53.7 1.3 %multiply_convert_fusion.2 = bf16[1024,512]{0,1:T(8,128)(2,1)S(1)} fusion(bf16[1024,512]{0,1:T(8,128)(2,1)S(1)} %copy.18, bf16[1024,512]{0,1:T(8,128)(2,1)S(1)} %get-tuple-element.55, bf16[512,512]{1,0:T(8,128)(2,1)S(1)} %bitcast.92), kind=kOutput, calls=%fused_computation.13 | convolution fusion | flops 542638080 | bytes 3670016 | tf_op jit(solution)/shard_map/dot_general | solution.py:622
  55.0 1.1 multiply_convert_fusion.1
  56.1 1.2 %multiply_convert_fusion = bf16[1024,512]{0,1:T(8,128)(2,1)S(1)} fusion(f32[1024,512]{0,1:T(8,128)S(1)} %get-tuple-element.54, bf16[1024,512]{0,1:T(8,128)(2,1)S(1)} %copy.18, bf16[512,512]{1,0:T(8,128)(2,1)S(1)} %bitcast.91, bf16[1024,512]{0,1:T(8,128)(2,1)S(1)} %multiply_convert_fusion.1), kind=kOutput, calls=%fused_computation.11 | convolution fusion | flops 543162368 | bytes 5767168 | tf_op jit(solution)/shard_map/ed,fd->ef/dot_general | solution.py:627
  57.3 1.5 %convolution_convert_fusion.2 = bf16[512,512]{1,0:T(8,128)(2,1)} fusion(bf16[1024,512]{0,1:T(8,128)(2,1)S(1)} %get-tuple-element.53, bf16[1024,512]{0,1:T(8,128)(2,1)S(1)} %multiply_convert_fusion.1), kind=kOutput, calls=%fused_computation.21 | convolution fusion | flops 537133056 | bytes 2621440 | tf_op jit(solution)/shard_map/ed,ef->df/dot_general | solution.py:633
  58.8 0.0 copy-start.2
  58.8 0.0 copy-start.4
  58.8 1.5 %convolution_convert_fusion.3 = bf16[512,512]{1,0:T(8,128)(2,1)} fusion(bf16[1024,512]{0,1:T(8,128)(2,1)S(1)} %get-tuple-element.55, bf16[1024,512]{0,1:T(8,128)(2,1)S(1)} %multiply_convert_fusion.2), kind=kOutput, calls=%fused_computation.22 | convolution fusion | flops 537133056 | bytes 2621440 | tf_op jit(solution)/shard_map/ed,ef->df/dot_general | solution.py:632
  60.4 0.0 copy-done.2
  60.4 1.1 fusion.8.refs_8_
  61.4 0.0 copy-done.4
  61.4 1.0 convolution_convert_fusion.4.refs_5_
  62.4 27.7 %backward_triplets.1 = (bf16[64,1024]{1,0:T(8,128)(2,1)}, f32[16,64]{1,0:T(8,128)}, bf16[4,16,512]{2,1,0:T(8,128)(2,1)}, bf16[4,16,512]{2,1,0:T(8,128)(2,1)}, bf16[4,8,512]{2,1,0:T(8,128)(2,1)}) custom-call(s32[1,8192]{1,0:T(1,128)} %bitcast.80, s32[1,8192]{1,0:T(1,128)} %bitcast.82, bf16[16,8192]{1,0:T(8,128)(2,1)} %refs_2_.3, bf16[16,64]{1,0:T(8,128)(2,1)} %bitcast.86, ...), custom_call_target="tpu_custom_call" | custom-call | tf_op jit(solution)/shard_map/backward_triplets/pallas_call | solution.py:551
  90.1 0.0 copy-start.3
  90.1 2.5 %fusion.7 = bf16[1024,512]{0,1:T(8,128)(2,1)S(1)} fusion(f32[512,1024]{1,0:T(8,128)} %get-tuple-element.52, bf16[512,64]{1,0:T(8,128)(2,1)S(1)} %bitcast.84, bf16[64,1024]{1,0:T(8,128)(2,1)} %get-tuple-element.37), kind=kOutput, calls=%fused_computation.10 | convolution fusion | flops 71827456 | bytes 3342336 | tf_op jit(solution)/shard_map/ke,dk->ed/dot_general | solution.py:649
  92.7 0.0 copy-done.3
  92.7 0.4 convolution_convert_fusion.6
  93.1 0.0 copy-start.5
  93.1 0.8 copy.30
  93.9 1.5 %convolution_convert_fusion.1 = bf16[512,512]{0,1:T(8,128)(2,1)} fusion(bf16[1024,512]{0,1:T(8,128)(2,1)S(1)} %fusion.7, bf16[1024,512]{1,0:T(8,128)(2,1)S(1)} %copy-done), kind=kOutput, calls=%fused_computation.20 | convolution fusion | flops 537133056 | bytes 2621440 | tf_op jit(solution)/shard_map/ed,ef->df/dot_general | solution.py:651
  95.4 0.0 copy-done.5
  95.4 1.7 %convolution_convert_fusion = bf16[1024,512]{1,0:T(8,128)(2,1)} fusion(bf16[1024,512]{0,1:T(8,128)(2,1)S(1)} %fusion.7, bf16[512,512]{1,0:T(8,128)(2,1)S(1)} %bitcast.89), kind=kOutput, calls=%fused_computation.19 | convolution fusion | flops 537395200 | bytes 2621440 | tf_op jit(solution)/shard_map/ef,df->ed/dot_general | solution.py:652
  97.2 18.3 %total_grads.1 = (bf16[4,16,512]{2,1,0:T(8,128)(2,1)}, bf16[4,64,64]{2,1,0:T(8,128)(2,1)}, f32[4,2,64]{2,1,0:T(2,128)}) custom-call(bf16[8,4,16,512]{3,2,1,0:T(8,128)(2,1)} %bitcast.77, bf16[8,64,64]{2,1,0:T(8,128)(2,1)} %bitcast.78, f32[8,2,64]{2,1,0:T(2,128)} %bitcast.87), custom_call_target="tpu_custom_call" | custom-call | tf_op jit(solution)/shard_map/total_grads/pallas_call | solution.py:318
  115.5 1.7 %write_grads.1 = (f32[64,512]{1,0:T(8,128)}, f32[64,64]{1,0:T(8,128)}, f32[2,64]{1,0:T(2,128)}, f32[8,512]{1,0:T(8,128)}, f32[64,512]{1,0:T(8,128)}, /*index=5*/f32[64,512]{1,0:T(8,128)}) custom-call(bf16[4,16,512]{2,1,0:T(8,128)(2,1)} %get-tuple-element.39.refs_0_, bf16[4,64,64]{2,1,0:T(8,128)(2,1)} %get-tuple-element.40.refs_1_, ...), custom_call_target="tpu_custom_call" | custom-call | tf_op jit(solution)/shard_map/write_grads/pallas_call | solution.py:343
Async XLA Ops:
  0.6 19.7 %copy-start = (bf16[1024,512]{1,0:T(8,128)(2,1)S(1)}, bf16[1024,512]{1,0:T(8,128)(2,1)}, u32[]{:S(2)}) copy-start(bf16[1024,512]{1,0:T(8,128)(2,1)} %param.11) | copy-start | bytes 3145732
  20.3 3.4 %copy-start.1 = (bf16[8,64,64]{2,1,0:T(8,128)(2,1)S(1)}, bf16[8,64,64]{2,1,0:T(8,128)(2,1)}, u32[]{:S(2)}) copy-start(bf16[8,64,64]{2,1,0:T(8,128)(2,1)} %get-tuple-element.30) | copy-start | bytes 196612
  50.9 1.7 %copy-start.6 = (bf16[8,64,512]{2,1,0:T(8,128)(2,1)S(1)}, bf16[8,64,512]{2,1,0:T(8,128)(2,1)}, u32[]{:S(2)}) copy-start(bf16[8,64,512]{2,1,0:T(8,128)(2,1)} %get-tuple-element.35) | copy-start | bytes 1572868
  52.6 1.1 copy-start.7
  58.8 1.5 %copy-start.2 = (bf16[64,1024]{1,0:T(8,128)(2,1)S(1)}, bf16[64,1024]{1,0:T(8,128)(2,1)}, u32[]{:S(2)}) copy-start(bf16[64,1024]{1,0:T(8,128)(2,1)} %get-tuple-element.34) | copy-start | bytes 393220
  58.8 2.6 %copy-start.4 = (bf16[8,8,512]{2,1,0:T(8,128)(2,1)S(1)}, bf16[8,8,512]{2,1,0:T(8,128)(2,1)}, u32[]{:S(2)}) copy-start(bf16[8,8,512]{2,1,0:T(8,128)(2,1)} %get-tuple-element.33) | copy-start | bytes 196612
  90.1 2.5 %copy-start.3 = (bf16[64,1024]{1,0:T(8,128)(2,1)S(1)}, bf16[64,1024]{1,0:T(8,128)(2,1)}, u32[]{:S(2)}) copy-start(bf16[64,1024]{1,0:T(8,128)(2,1)} %get-tuple-element.37) | copy-start | bytes 393220
  93.1 2.3 %copy-start.5 = (bf16[8,64,512]{2,1,0:T(8,128)(2,1)S(1)}, bf16[8,64,512]{2,1,0:T(8,128)(2,1)}, u32[]{:S(2)}) copy-start(bf16[8,64,512]{2,1,0:T(8,128)(2,1)} %get-tuple-element.31) | copy-start | bytes 1572868

commit v3 on v2

--- a/solution.py
+++ b/solution.py
@@ -448,14 +448,14 @@
         return carry
 
     next(steps)
+    next(steps, None)
     for cp in copies:
         cp.wait()
     tiles = trips // tile
-    count = n // 2 - 1
+    count = max(n // 2 - 2, 1)
     for i in range(count):
-        lax.fori_loop(tiles * i // (count + 1), tiles * (i + 1) // (count + 1), work, 0)
-        next(steps)
-    lax.fori_loop(tiles * count // (count + 1), tiles, work, 0)
+        next(steps, None)
+        lax.fori_loop(tiles * i // count, tiles * (i + 1) // count, work, 0)
     for h in range(subs):
         agg_ref[:, h * SUB : (h + 1) * SUB] = acc[h * width : (h + 1) * width, :].astype(BF16)
     for _ in steps:
@@ -524,9 +524,10 @@
         return carry
 
     tiles = trips // tile
-    for i in range(4):
+    cuts = (0, tiles // 8, tiles * 5 // 8, tiles * 7 // 8, tiles)
+    for low, high in zip(cuts[:-1], cuts[1:]):
         next(steps)
-        lax.fori_loop(tiles * i // 4, tiles * (i + 1) // 4, work, 0)
+        lax.fori_loop(low, high, work, 0)
     for g in range(groups):
         part[g] = acc[g * width : (g + 1) * width, :].astype(BF16)
     copies = []

time: 118 us -> 117 us (level)
    pallas_call x1, Pallas kernels: 26.2 us -> 25 us  [forward_triplets(): pl.pallas_call(functools.partial(forward_kernel, n, groups), out_shape=[j...]
where the time goes in v3:
time: 117 us
  Pallas kernels  91.6 us (78%)
  matrix products  22.1 us (19%)
  local copies, waits for them, and re-layouts  2.29 us (2%)
    pallas_call x1, Pallas kernels, backward_triplets(): pl.pallas_call(functools.partial(backward_kernel, n, groups, kinds), out_...  27.8 us
    pallas_call x1, Pallas kernels, forward_triplets(): pl.pallas_call(functools.partial(forward_kernel, n, groups), out_shape=[j...  25 us
    pallas_call x1, Pallas kernels, total_grads(): pl.pallas_call(functools.partial(total_kernel, n, groups, kinds), out_sha...  18.8 us
    pallas_call x1, Pallas kernels, gather_weights(): pl.pallas_call(functools.partial(gather_kernel, n, count), out_shape=gath...  18.2 us
    dot_general x1, matrix products, on_device(): z_one = jnp.dot(edge_feats, w_pair, preferred_element_type=F32)  3.39 us
    dot_general x1, matrix products, on_device(): jnp.einsum('ke,dk->ed', ddown_t, w_down, preferred_element_type=F32)  2.53 us

profile of v3, /device:TPU:0, one launch (start us, length us, event | category | flops | bytes accessed | tf_op | source)
XLA Modules:
  0.0 116.7 jit_solution(881087604706676226)
XLA Ops:
  0.6 0.0 copy-start
  0.6 18.2 %gather_weights.1 = (bf16[8,64,512]{2,1,0:T(8,128)(2,1)}, bf16[8,64,64]{2,1,0:T(8,128)(2,1)}, bf16[8,2,64]{2,1,0:T(2,128)(2,1)}) custom-call(bf16[64,512]{1,0:T(8,128)(2,1)} %refs_0_.1, bf16[64,64]{1,0:T(8,128)(2,1)} %refs_1_.1, bf16[2,64]{1,0:T(2,128)(2,1)} %refs_2_.2), custom_call_target="tpu_custom_call" | custom-call | tf_op jit(solution)/shard_map/gather_weights/pallas_call | solution.py:147
  18.8 1.5 %copy.18 = bf16[1024,512]{0,1:T(8,128)(2,1)S(1)} copy(bf16[1024,512]{1,0:T(8,128)(2,1)} %param.12) | data formatting | bytes 2097152 | tf_op args[1]
  20.3 0.0 copy-done
  20.3 0.0 copy-start.1
  20.3 3.4 %fusion.3 = (bf16[1024,512]{0,1:T(8,128)(2,1)S(1)}, f32[512,1024]{1,0:T(8,128)}) fusion(bf16[512,512]{1,0:T(8,128)(2,1)} %bitcast.88, bf16[1024,512]{1,0:T(8,128)(2,1)S(1)} %copy-done), kind=kOutput, calls=%fused_computation.6 | convolution fusion | flops 539492352 | bytes 4718592 | tf_op jit(solution)/shard_map/dot_general | solution.py:605
  23.7 0.0 copy-done.1
  23.7 1.0 convolution_convert_fusion.5.down_ref
  24.7 25.0 %forward_triplets.1 = (bf16[64,1024]{1,0:T(8,128)(2,1)}, bf16[64,8192]{1,0:T(8,128)(2,1)}, bf16[8,8,512]{2,1,0:T(8,128)(2,1)}, bf16[8,64,512]{2,1,0:T(8,128)(2,1)}, bf16[8,64,512]{2,1,0:T(8,128)(2,1)}) custom-call(s32[1,8192]{1,0:T(1,128)} %bitcast.79, s32[1,8192]{1,0:T(1,128)} %bitcast.81, bf16[16,8192]{1,0:T(8,128)(2,1)} %refs_2_.3, ...), custom_call_target="tpu_custom_call" | custom-call | tf_op jit(solution)/shard_map/forward_triplets/pallas_call | solution.py:468
  49.7 0.0 copy-start.6
  49.7 1.7 %multiply_convert_fusion.4 = (bf16[1024,512]{0,1:T(8,128)(2,1)S(1)}, f32[1024,512]{0,1:T(8,128)S(1)}) fusion(bf16[64,1024]{1,0:T(8,128)(2,1)} %get-tuple-element.34, bf16[8,8,512]{2,1,0:T(8,128)(2,1)} %get-tuple-element.33), kind=kOutput, calls=%fused_computation.16 | convolution fusion | flops 69730304 | bytes 3342336 | tf_op jit(solution)/shard_map/ke,kd->ed/dot_general | solution.py:619
  51.4 0.0 copy-done.6
  51.4 0.0 copy-start.7
  51.4 1.0 multiply_convert_fusion.3
  52.5 0.0 copy-done.7
  52.5 1.3 %multiply_convert_fusion.2 = bf16[1024,512]{0,1:T(8,128)(2,1)S(1)} fusion(bf16[1024,512]{0,1:T(8,128)(2,1)S(1)} %copy.18, bf16[1024,512]{0,1:T(8,128)(2,1)S(1)} %get-tuple-element.55, bf16[512,512]{1,0:T(8,128)(2,1)S(1)} %bitcast.92), kind=kOutput, calls=%fused_computation.13 | convolution fusion | flops 542638080 | bytes 3670016 | tf_op jit(solution)/shard_map/dot_general | solution.py:623
  53.8 1.1 multiply_convert_fusion.1
  54.9 1.2 %multiply_convert_fusion = bf16[1024,512]{0,1:T(8,128)(2,1)S(1)} fusion(f32[1024,512]{0,1:T(8,128)S(1)} %get-tuple-element.54, bf16[1024,512]{0,1:T(8,128)(2,1)S(1)} %copy.18, bf16[512,512]{1,0:T(8,128)(2,1)S(1)} %bitcast.91, bf16[1024,512]{0,1:T(8,128)(2,1)S(1)} %multiply_convert_fusion.1), kind=kOutput, calls=%fused_computation.11 | convolution fusion | flops 543162368 | bytes 5767168 | tf_op jit(solution)/shard_map/ed,fd->ef/dot_general | solution.py:628
  56.1 1.5 %convolution_convert_fusion.2 = bf16[512,512]{1,0:T(8,128)(2,1)} fusion(bf16[1024,512]{0,1:T(8,128)(2,1)S(1)} %get-tuple-element.53, bf16[1024,512]{0,1:T(8,128)(2,1)S(1)} %multiply_convert_fusion.1), kind=kOutput, calls=%fused_computation.21 | convolution fusion | flops 537133056 | bytes 2621440 | tf_op jit(solution)/shard_map/ed,ef->df/dot_general | solution.py:634
  57.6 0.0 copy-start.2
  57.6 0.0 copy-start.4
  57.6 1.5 %convolution_convert_fusion.3 = bf16[512,512]{1,0:T(8,128)(2,1)} fusion(bf16[1024,512]{0,1:T(8,128)(2,1)S(1)} %get-tuple-element.55, bf16[1024,512]{0,1:T(8,128)(2,1)S(1)} %multiply_convert_fusion.2), kind=kOutput, calls=%fused_computation.22 | convolution fusion | flops 537133056 | bytes 2621440 | tf_op jit(solution)/shard_map/ed,ef->df/dot_general | solution.py:633
  59.2 0.0 copy-done.2
  59.2 1.1 fusion.8.refs_8_
  60.3 0.0 copy-done.4
  60.3 1.0 convolution_convert_fusion.4.refs_5_
  61.2 27.8 %backward_triplets.1 = (bf16[64,1024]{1,0:T(8,128)(2,1)}, f32[16,64]{1,0:T(8,128)}, bf16[4,16,512]{2,1,0:T(8,128)(2,1)}, bf16[4,16,512]{2,1,0:T(8,128)(2,1)}, bf16[4,8,512]{2,1,0:T(8,128)(2,1)}) custom-call(s32[1,8192]{1,0:T(1,128)} %bitcast.80, s32[1,8192]{1,0:T(1,128)} %bitcast.82, bf16[16,8192]{1,0:T(8,128)(2,1)} %refs_2_.3, bf16[16,64]{1,0:T(8,128)(2,1)} %bitcast.86, ...), custom_call_target="tpu_custom_call" | custom-call | tf_op jit(solution)/shard_map/backward_triplets/pallas_call | solution.py:552
  89.1 0.0 copy-start.3
  89.1 2.5 %fusion.7 = bf16[1024,512]{0,1:T(8,128)(2,1)S(1)} fusion(f32[512,1024]{1,0:T(8,128)} %get-tuple-element.52, bf16[512,64]{1,0:T(8,128)(2,1)S(1)} %bitcast.84, bf16[64,1024]{1,0:T(8,128)(2,1)} %get-tuple-element.37), kind=kOutput, calls=%fused_computation.10 | convolution fusion | flops 71827456 | bytes 3342336 | tf_op jit(solution)/shard_map/ke,dk->ed/dot_general | solution.py:650
  91.6 0.0 copy-done.3
  91.6 0.4 convolution_convert_fusion.6
  92.1 0.0 copy-start.5
  92.1 0.8 copy.30
  92.8 1.5 %convolution_convert_fusion.1 = bf16[512,512]{0,1:T(8,128)(2,1)} fusion(bf16[1024,512]{0,1:T(8,128)(2,1)S(1)} %fusion.7, bf16[1024,512]{1,0:T(8,128)(2,1)S(1)} %copy-done), kind=kOutput, calls=%fused_computation.20 | convolution fusion | flops 537133056 | bytes 2621440 | tf_op jit(solution)/shard_map/ed,ef->df/dot_general | solution.py:652
  94.4 0.0 copy-done.5
  94.4 1.7 %convolution_convert_fusion = bf16[1024,512]{1,0:T(8,128)(2,1)} fusion(bf16[1024,512]{0,1:T(8,128)(2,1)S(1)} %fusion.7, bf16[512,512]{1,0:T(8,128)(2,1)S(1)} %bitcast.89), kind=kOutput, calls=%fused_computation.19 | convolution fusion | flops 537395200 | bytes 2621440 | tf_op jit(solution)/shard_map/ef,df->ed/dot_general | solution.py:653
  96.1 18.8 %total_grads.1 = (bf16[4,16,512]{2,1,0:T(8,128)(2,1)}, bf16[4,64,64]{2,1,0:T(8,128)(2,1)}, f32[4,2,64]{2,1,0:T(2,128)}) custom-call(bf16[8,4,16,512]{3,2,1,0:T(8,128)(2,1)} %bitcast.77, bf16[8,64,64]{2,1,0:T(8,128)(2,1)} %bitcast.78, f32[8,2,64]{2,1,0:T(2,128)} %bitcast.87), custom_call_target="tpu_custom_call" | custom-call | tf_op jit(solution)/shard_map/total_grads/pallas_call | solution.py:318
  115.0 1.7 %write_grads.1 = (f32[64,512]{1,0:T(8,128)}, f32[64,64]{1,0:T(8,128)}, f32[2,64]{1,0:T(2,128)}, f32[8,512]{1,0:T(8,128)}, f32[64,512]{1,0:T(8,128)}, /*index=5*/f32[64,512]{1,0:T(8,128)}) custom-call(bf16[4,16,512]{2,1,0:T(8,128)(2,1)} %get-tuple-element.39.refs_0_, bf16[4,64,64]{2,1,0:T(8,128)(2,1)} %get-tuple-element.40.refs_1_, ...), custom_call_target="tpu_custom_call" | custom-call | tf_op jit(solution)/shard_map/write_grads/pallas_call | solution.py:343
Async XLA Ops:
  0.6 19.7 %copy-start = (bf16[1024,512]{1,0:T(8,128)(2,1)S(1)}, bf16[1024,512]{1,0:T(8,128)(2,1)}, u32[]{:S(2)}) copy-start(bf16[1024,512]{1,0:T(8,128)(2,1)} %param.11) | copy-start | bytes 3145732
  20.3 3.4 %copy-start.1 = (bf16[8,64,64]{2,1,0:T(8,128)(2,1)S(1)}, bf16[8,64,64]{2,1,0:T(8,128)(2,1)}, u32[]{:S(2)}) copy-start(bf16[8,64,64]{2,1,0:T(8,128)(2,1)} %get-tuple-element.30) | copy-start | bytes 196612
  49.7 1.7 %copy-start.6 = (bf16[8,64,512]{2,1,0:T(8,128)(2,1)S(1)}, bf16[8,64,512]{2,1,0:T(8,128)(2,1)}, u32[]{:S(2)}) copy-start(bf16[8,64,512]{2,1,0:T(8,128)(2,1)} %get-tuple-element.35) | copy-start | bytes 1572868
  51.4 1.1 copy-start.7
  57.6 1.5 %copy-start.2 = (bf16[64,1024]{1,0:T(8,128)(2,1)S(1)}, bf16[64,1024]{1,0:T(8,128)(2,1)}, u32[]{:S(2)}) copy-start(bf16[64,1024]{1,0:T(8,128)(2,1)} %get-tuple-element.34) | copy-start | bytes 393220
  57.6 2.6 %copy-start.4 = (bf16[8,8,512]{2,1,0:T(8,128)(2,1)S(1)}, bf16[8,8,512]{2,1,0:T(8,128)(2,1)}, u32[]{:S(2)}) copy-start(bf16[8,8,512]{2,1,0:T(8,128)(2,1)} %get-tuple-element.33) | copy-start | bytes 196612
  89.1 2.5 %copy-start.3 = (bf16[64,1024]{1,0:T(8,128)(2,1)S(1)}, bf16[64,1024]{1,0:T(8,128)(2,1)}, u32[]{:S(2)}) copy-start(bf16[64,1024]{1,0:T(8,128)(2,1)} %get-tuple-element.37) | copy-start | bytes 393220
  92.1 2.3 %copy-start.5 = (bf16[8,64,512]{2,1,0:T(8,128)(2,1)S(1)}, bf16[8,64,512]{2,1,0:T(8,128)(2,1)}, u32[]{:S(2)}) copy-start(bf16[8,64,512]{2,1,0:T(8,128)(2,1)} %get-tuple-element.31) | copy-start | bytes 1572868
